TPU v7x, 128 devices: a whole 4x4x4 slice. The times are simulated.
128 devices in a mesh: row: 16 (over y, x), col: 8 (over z, core).
Axes of the slice: x: 4, y: 4, z: 4, core: 2. Of those that a mesh axis runs over, the one named last changes fastest.
Arguments:
- orbitals: float32 [32768, 1024], P('row', 'col'), may hold values from -6 to 6
- point_index: int32 [8192], replicated, may hold values from 0 to 32767, as said below
- coulomb: float32 [8192, 8192], P('row', 'col'), may hold values from -0.001953125 to 0.001953125
- fitting: float32 [32768, 8192], P('row', 'col'), may hold values from -0.0625 to 0.0625
Outputs:
- exchange_out: float32 [32768, 1024], P('row', 'col')
Inputs may be any that keep to these rules, and one draw needn't show every extreme that they name: `point_index`: indices are distinct. Grid index g lies in slab g // 2048. Of the 512 consecutive points of each row panel, at most 64 lie in one slab, and in every panel exactly 64 lie in one slab.
All inputs are finite; a program needn't handle non-finite values.
Results may differ from a plain program's by a relative error of at most 0.00012.
Values sent between devices are 32-bit elements; how exact they have to be, the bound alone decides.
No kernel may reach another device: no remote copies, remote signals or barrier semaphores. Data moves between devices by JAX's collectives and lax.ppermute only.
A program may use at most 64 MiB of HBM per device.

v0:
```python
import functools

import jax
import jax.numpy as jnp
from jax import lax
from jax.experimental import pallas as pl
from jax.experimental.pallas import tpu as pltpu
from jax.sharding import PartitionSpec as P


SIDE = 4
REL = (0, -1, 1, 2)
F32 = jnp.float32
BF16 = jnp.bfloat16


def shift(axis, step):
    pairs = []
    if axis == "z":
        for z in range(SIDE):
            for k in range(2):
                pairs.append((z * 2 + k, ((z + step) % SIDE) * 2 + k))
        return "col", pairs
    for y in range(SIDE):
        for x in range(SIDE):
            ty = (y + step) % SIDE if axis == "y" else y
            tx = (x + step) % SIDE if axis == "x" else x
            pairs.append((y * SIDE + x, ty * SIDE + tx))
    return "row", pairs


def move(value, axis, step):
    name, pairs = shift(axis, step)
    return lax.ppermute(value, name, pairs)


def swap_cores(value):
    return lax.ppermute(value, "col", [(c, c ^ 1) for c in range(2 * SIDE)])


def scatter_pairs(turn):
    pairs = []
    for y in range(SIDE):
        for x in range(SIDE):
            for z in range(SIDE):
                for k in range(2):
                    strip = (z + turn) % SIDE
                    ty = ((strip if k == 0 else -strip) - y) % SIDE
                    tx = x if k == 0 else x ^ 3
                    target = (ty * SIDE + tx) * 8 + y * 2 + (x >> 1)
                    pairs.append(((y * SIDE + x) * 8 + z * 2 + k, target))
    return pairs


def to_plane(value, turn):
    return lax.ppermute(value, ("row", "col"), scatter_pairs(turn))


def gather_line(low, high, axis):
    before_low, after_high = move(low, axis, 1), move(high, axis, -1)
    before_high, after_low = move(high, axis, 1), move(low, axis, -1)
    far_low, far_high = move(before_low, axis, 1), move(after_high, axis, -1)
    return low, high, before_low, before_high, after_low, after_high, far_low, far_high


def line_halves(block, axis):
    before, after, far = move(block, axis, 1), move(block, axis, -1), move(block, axis, 2)
    return jnp.stack([block, before]), jnp.stack([after, far])


def gather_plane(block):
    half = block.shape[0] // 2
    first = line_halves(block[:half], "x")
    second = line_halves(block[half:], "y")
    return gather_line(*first, "y") + gather_line(*second, "x")


def plane_order(my_row, my_col):
    rel = jnp.array(REL, jnp.int32)
    y, x = my_row // SIDE, my_row % SIDE
    z, k = my_col // 2, my_col % 2
    outer, inner = jnp.repeat(rel, SIDE), jnp.tile(rel, SIDE)

    def describe(dy, dx):
        py, px = (y + dy) % SIDE, (x + dx) % SIDE
        strip_k = (px >> 1) ^ k
        panel = (px & 1) ^ strip_k
        return panel, (jnp.where(strip_k == 0, py + z, -py - z) % SIDE) * 2 + strip_k

    first, second = describe(outer, inner), describe(inner, outer)
    return jnp.stack([first[0], first[1], second[0], second[1]])


def split(value):
    high = value.astype(BF16)
    return high, (value - high.astype(F32)).astype(BF16)


def dot3(a_high, a_low, b_high, b_low, dims):
    dot = functools.partial(
        lax.dot_general, dimension_numbers=(dims, ((), ())), preferred_element_type=F32
    )
    return dot(a_high, b_high) + (dot(a_high, b_low) + dot(a_low, b_high))


def piece_blocks(pieces):
    found, position = [], 0
    for ref in pieces:
        for block in range(ref.shape[0]):
            found.append((ref, block, position))
            position += 1
    return found


def pair_kernel(order, panel_order, chips, *refs):
    first, second, panels = refs[:8], refs[8:16], refs[16:24]
    coulomb_in, keep, send = refs[24:27]
    column, panel, p_high, p_low, c_high, c_low, t_high, t_low, total, coulomb, column_sem, panel_sem = refs[27:]
    rows = first[0].shape[1]
    lanes = first[0].shape[2]
    panel_copies = [pltpu.make_async_copy(coulomb_in, coulomb, panel_sem.at[8])]
    for ref, block, position in piece_blocks(panels):
        lane = pl.multiple_of(panel_order[position] * lanes, lanes)
        panel_copies.append(
            pltpu.make_async_copy(ref.at[block], panel.at[:, pl.ds(lane, lanes)], panel_sem.at[position])
        )
        panel_copies[-1].start()
    panel_copies[0].start()
    for which, pieces in enumerate((first, second)):
        for ref, block, position in piece_blocks(pieces):
            part = order[2 * which, position] * 2 + which
            strip = order[2 * which + 1, position]
            row = pl.multiple_of(part * rows, rows)
            lane = pl.multiple_of(strip * lanes, lanes)
            pltpu.make_async_copy(
                ref.at[block],
                column.at[pl.ds(row, rows), pl.ds(lane, lanes)],
                column_sem.at[part * 8 + strip],
            ).start()
    for copy in panel_copies:
        copy.wait()
    p_high[...], p_low[...] = split(panel[...])

    @pl.loop(0, 4)
    def _(step):
        part = lax.rem(step, 2) * 2 + step // 2
        here = pl.ds(pl.multiple_of(part * rows, rows), rows)
        for strip in range(8):
            pltpu.make_async_copy(
                first[0].at[0], column.at[here, pl.ds(strip * lanes, lanes)], column_sem.at[part * 8 + strip]
            ).wait()
        high, low = split(column[here, :])
        c_high[here, :], c_low[here, :] = high, low
        pair = dot3(p_high[...], p_low[...], high, low, ((1,), (1,)))
        t_high[:, here], t_low[:, here] = split(coulomb[:, here] * pair)

    @pl.loop(0, 4)
    def _(step):
        here = pl.ds(pl.multiple_of(step * 256, 256), 256)
        total[:, here] = dot3(t_high[...], t_low[...], c_high[:, here], c_low[:, here], ((1,), (0,)))

    core, height = chips[4], chips[3]
    count = keep.shape[1]
    for turn in range(SIDE):
        strip = lax.rem(height + turn, SIDE) * 2
        keep[turn] = total[pl.ds(pl.multiple_of((strip + core) * count, count), count), :]
        send[turn] = total[pl.ds(pl.multiple_of((strip + 1 - core) * count, count), count), :]


def pair_weights(order, panel_order, chips, column_pieces, panel_pieces, coulomb):
    rows, width = coulomb.shape
    bands = 8 * 128
    anywhere = pl.BlockSpec(memory_space=pl.ANY)
    scalars = pl.BlockSpec(memory_space=pltpu.SMEM)
    vmem = pl.BlockSpec(memory_space=pltpu.VMEM)
    out = jax.ShapeDtypeStruct((SIDE, rows // 8, bands), F32)
    return pl.pallas_call(
        pair_kernel,
        out_shape=(out, out),
        in_specs=[scalars, scalars, scalars] + [anywhere] * 24 + [pl.BlockSpec(memory_space=pltpu.HBM)],
        out_specs=(vmem, vmem),
        scratch_shapes=[
            pltpu.VMEM((width, bands), F32),
            pltpu.VMEM((rows, bands), F32),
            pltpu.VMEM((rows, bands), BF16),
            pltpu.VMEM((rows, bands), BF16),
            pltpu.VMEM((width, bands), BF16),
            pltpu.VMEM((width, bands), BF16),
            pltpu.VMEM((rows, width), BF16),
            pltpu.VMEM((rows, width), BF16),
            pltpu.VMEM((rows, bands), F32),
            pltpu.VMEM((rows, width), F32),
            pltpu.SemaphoreType.DMA((32,)),
            pltpu.SemaphoreType.DMA((9,)),
        ],
        compiler_params=pltpu.CompilerParams(vmem_limit_bytes=32 << 20),
        cost_estimate=pl.CostEstimate(flops=12 * rows * width * bands, bytes_accessed=12 << 20, transcendentals=0),
        name="pair_weights",
    )(order, panel_order, chips, *column_pieces, *panel_pieces, pltpu.with_memory_space_constraint(coulomb, pltpu.HBM))


def term_kernel(gathered, where, *refs):
    tile = pl.program_id(0)
    if gathered:
        order, first, second = refs[0], refs[1:9], refs[9:17]
        fitting, outs, high_out, low_out, high, low, whole, sem = refs[17], refs[18:22], *refs[22:]
        kept = [
            pltpu.make_async_copy(high, high_out, sem.at[32]),
            pltpu.make_async_copy(low, low_out, sem.at[33]),
        ]

        @pl.when(tile == 0)
        def _():
            rows = first[0].shape[1]
            copies = []
            for which, pieces in enumerate((first, second)):
                for ref, block, position in piece_blocks(pieces):
                    strip = order[2 * which, position] * 8 + order[2 * which + 1, position]
                    row = pl.multiple_of((strip * 2 + which) * rows, rows)
                    copies.append(
                        pltpu.make_async_copy(
                            ref.at[block], whole.at[pl.ds(row, rows), :], sem.at[which * 16 + position]
                        )
                    )
            for copy in copies:
                copy.start()
            for copy in copies:
                copy.wait()
            high[...], low[...] = split(whole[...])
            for copy in kept:
                copy.start()

        @pl.when(tile == pl.num_programs(0) - 1)
        def _():
            for copy in kept:
                copy.wait()
    else:
        fitting, weights, outs = refs[0], refs[1:5], refs[7:11]
    f_high, f_low = split(fitting[...])
    even = where[4] == 0
    half = outs[0].shape[2]
    for group in range(2):
        if gathered:
            start = chip_of(True, group, tile, where) * 2 * half
            here = pl.ds(pl.multiple_of(start, 2 * half), 2 * half)
            w_high, w_low = high[:, here], low[:, here]
        else:
            w_high, w_low = weights[2 * group][...], weights[2 * group + 1][...]
        product = dot3(f_high, f_low, w_high, w_low, ((1,), (0,)))
        lower, upper = product[:, :half], product[:, half:]
        outs[2 * group][0] = jnp.where(even, lower, upper)
        outs[2 * group + 1][0] = jnp.where(even, upper, lower)


def chip_of(gathered, group, tile, where):
    if group == 0:
        return where[0] if gathered else where[3]
    return jnp.where((tile < 2) == gathered, where[1], where[2])


def term(where, fitting, gathered=None, weights=None, after=None):
    rows, points = fitting.shape
    bands = 8 * 128
    tile = rows // 4
    anywhere = pl.BlockSpec(memory_space=pltpu.HBM)
    streamed = pl.BlockSpec((tile, points), lambda i, where: (i, 0))
    half = pl.BlockSpec((1, tile, bands // 8), lambda i, where: (i // 2, lax.rem(i, 2), 0))
    out = [jax.ShapeDtypeStruct((2, rows // 2, bands // 8), F32)] * 4
    out_specs = [half] * 4
    scratch = []
    if gathered is not None:
        in_specs = [pl.BlockSpec(memory_space=pltpu.SMEM)] + [anywhere] * 16 + [streamed]
        operands = (*gathered, fitting)
        out += [jax.ShapeDtypeStruct((points, bands), BF16)] * 2
        out_specs += [anywhere] * 2
        scratch = [pltpu.VMEM((points, bands), BF16)] * 2
        scratch += [pltpu.VMEM((points, bands), F32), pltpu.SemaphoreType.DMA((34,))]
    else:
        in_specs = [streamed]
        for group in range(2):
            chosen = pl.BlockSpec(
                (points, bands // SIDE), lambda i, where, group=group: (0, chip_of(False, group, i, where))
            )
            in_specs += [chosen, chosen]
        in_specs += [anywhere] * 2
        operands = (fitting, *weights, *weights, *after)
    return pl.pallas_call(
        functools.partial(term_kernel, gathered is not None),
        out_shape=out,
        grid_spec=pltpu.PrefetchScalarGridSpec(
            num_scalar_prefetch=1,
            grid=(rows // tile,),
            in_specs=in_specs,
            out_specs=out_specs,
            scratch_shapes=scratch,
        ),
        cost_estimate=pl.CostEstimate(
            flops=12 * rows * points * bands // SIDE, bytes_accessed=16 << 20, transcendentals=0
        ),
        name="term",
    )(where, *operands)


def picked_strip(orbitals, point_index, my_row):
    row_count = SIDE * SIDE
    slab_rows, lanes = orbitals.shape
    per_panel = point_index.shape[0] // row_count
    slot_count = 2 * per_panel // row_count
    owner = point_index // slab_rows
    owner_grid = owner.reshape(row_count, per_panel)
    local_grid = (point_index - owner * slab_rows).reshape(row_count, per_panel)
    spot = jnp.arange(per_panel)
    earlier = (spot[:, None] < spot[None, :]).astype(BF16)
    mine = owner_grid == my_row
    rank = jnp.dot(mine.astype(BF16), earlier, preferred_element_type=F32).astype(jnp.int32)
    chosen = mine[:, :, None] & (rank[:, :, None] == jnp.arange(slot_count)[None, None, :])
    source_row = jnp.sum(jnp.where(chosen, local_grid[:, :, None], 0), axis=1)
    outgoing = orbitals[source_row.reshape(-1)].reshape(row_count, slot_count, lanes)
    received = lax.all_to_all(outgoing, "row", split_axis=0, concat_axis=0, tiled=True)
    owner_mine = lax.dynamic_slice_in_dim(owner_grid, my_row, 1, 0)[0]
    matches = owner_mine[None, :] == jnp.arange(row_count)[:, None]
    ranks = jnp.dot(matches.astype(BF16), earlier, preferred_element_type=F32).astype(jnp.int32)
    slot_mine = jnp.sum(jnp.where(matches, ranks, 0), axis=0)
    return received.reshape(row_count * slot_count, lanes)[owner_mine * slot_count + slot_mine]


def exchange(orbitals, point_index, coulomb, fitting):
    my_row = lax.axis_index("row")
    my_col = lax.axis_index("col")
    height, core = my_col // 2, my_col % 2
    order = plane_order(my_row, my_col)
    strip = picked_strip(orbitals, point_index, my_row)

    column_pieces = gather_plane(to_plane(strip, 0))
    panel = strip.reshape((1,) + strip.shape)
    panel_pieces = gather_line(panel, swap_cores(panel), "z")
    chips = (height + jnp.array([2, -1, 1, 0], jnp.int32)) % SIDE
    chips = jnp.concatenate([chips, core[None]]).astype(jnp.int32)
    place = jnp.array(REL, jnp.int32).repeat(2)
    cores = jnp.tile(jnp.array([0, 1], jnp.int32), SIDE)
    panel_order = (((height + place) % SIDE) * 2 + (core ^ cores)).astype(jnp.int32)
    keep, send = pair_weights(order, panel_order, chips, column_pieces, panel_pieces, coulomb)

    summed = keep + swap_cores(send)
    parts = [to_plane(summed[turn], turn) for turn in range(SIDE)]
    w_strip = (parts[0] + parts[1]) + (parts[2] + parts[3])
    pieces = gather_plane(w_strip)

    def both_cores(mine, other):
        other = swap_cores(other)
        return mine[0] + other[0], mine[1] + other[1]

    mine_far, other_far, mine, other, *weights = term(chips, fitting, gathered=(order, *pieces))
    far_low, far_high = both_cores(mine_far, other_far)
    far_up = move(far_low, "z", 1)
    far_down = move(far_high, "z", -1)
    down_low, up_high = both_cores(mine, other)
    after = (down_low, up_high)
    up_high = move(up_high, "z", 1)
    down_low = move(down_low, "z", -1)
    mine_own, other_own, mine, other = term(chips, fitting, weights=weights, after=after)
    up_low, down_high = both_cores(mine, other)
    up_low = move(up_low + far_up, "z", 1)
    down_high = move(down_high + far_down, "z", -1)
    own_low, own_high = both_cores(mine_own, other_own)
    low = own_low + (up_low + down_low)
    high = own_high + (up_high + down_high)
    return -jnp.concatenate([low, high], axis=0)


def solution(mesh):
    in_specs = (P("row", "col"), P(), P("row", "col"), P("row", "col"))
    out_specs = P("row", "col")
    return jax.shard_map(exchange, mesh=mesh, in_specs=in_specs, out_specs=out_specs, check_vma=False)
```

profile of v0, /device:TPU:1, one launch (start us, length us, event | category | flops | bytes accessed | tf_op | source)
XLA Modules:
  0.0 246.8 jit_solution(5511028300506562516)
XLA Ops:
  1.8 4.0 %gather_fusion = f32[1024,128]{1,0:T(8,128)} fusion(f32[2048,128]{1,0:T(8,128)S(1)} %copy-done, s32[1024]{0:T(1024)S(1)} %broadcast_clamp_fusion), kind=kCustom, calls=%fused_computation | custom fusion | bytes 1052672 | tf_op jit(solution)/shard_map/gather | solution.py:318
  5.8 7.6 %all-to-all-start = ((f32[16,64,128]{2,1,0:T(8,128)}), f32[16,64,128]{2,1,0:T(8,128)S(1)}, u32[]{:S(2)}, u32[]{:S(2)}) async-start(f32[16,64,128]{2,1,0:T(8,128)} %bitcast.2), calls=%async_computation | async-start | bytes 1048576 | tf_op jit(solution)/shard_map/all_to_all | solution.py:319
  13.9 9.9 %all-to-all-done = f32[16,64,128]{2,1,0:T(8,128)S(1)} async-done(((f32[16,64,128]{2,1,0:T(8,128)}), f32[16,64,128]{2,1,0:T(8,128)S(1)}, u32[]{:S(2)}, u32[]{:S(2)}) %all-to-all-start) | async-done | bytes 524320 | tf_op jit(solution)/shard_map/all_to_all | solution.py:319
  23.8 1.0 gather_fusion.1
  24.9 4.1 %collective-permute-start = (f32[512,128]{1,0:T(8,128)S(1)}, f32[512,128]{1,0:T(8,128)S(1)}, u32[]{:S(2)}, u32[]{:S(2)}) collective-permute-start(f32[512,128]{1,0:T(8,128)S(1)} %gather_fusion.1), channel_id=1, source_target_pairs={{0,0},{1,24},{2,32},{3,120},{4,64},{5,88},{6,96},{7,56},{8,8},{9,1... | collective-permute-start | bytes 786440 | tf_op jit(solution)/shard_map/ppermute | solution.py:56
  29.1 2.4 collective-permute-start.22
  31.7 1.5 collective-permute-start.19
  33.6 1.2 collective-permute-start.1
  34.8 5.6 %collective-permute-done.22.refs_20_ = f32[1,512,128]{2,1,0:T(8,128)S(1)} collective-permute-done((f32[1,512,128]{2,1,0:T(8,128)S(1)}, f32[1,512,128]{2,1,0:T(8,128)S(1)}, u32[]{:S(2)}, u32[]{:S(2)}) %collective-permute-start.22) | collective-permute-done | bytes 262176 | tf_op jit(solution)/shard_map/ppermute | solution.py:34
  40.5 1.5 collective-permute-start.24
  42.0 5.8 %collective-permute-start.11 = (f32[256,128]{1,0:T(8,128)S(1)}, f32[256,128]{1,0:T(8,128)S(1)}, u32[]{:S(2)}, u32[]{:S(2)}) collective-permute-start(f32[256,128]{1,0:T(8,128)S(1)} %get-tuple-element.51), channel_id=1, source_target_pairs={{0,96},{8,104},{16,112},{24,120},{32,0},{40,8},{48,16},{56,24},{64... | collective-permute-start | bytes 393224 | tf_op jit(solution)/shard_map/ppermute | solution.py:34
  47.8 3.1 %collective-permute-start.12 = (f32[256,128]{1,0:T(8,128)S(1)}, f32[256,128]{1,0:T(8,128)S(1)}, u32[]{:S(2)}, u32[]{:S(2)}) collective-permute-start(f32[256,128]{1,0:T(8,128)S(1)} %get-tuple-element.51), channel_id=1, source_target_pairs={{0,64},{8,72},{16,80},{24,88},{32,96},{40,104},{48,112},{56,120},{... | collective-permute-start | bytes 393224 | tf_op jit(solution)/shard_map/ppermute | solution.py:34
  51.0 1.6 collective-permute-start.23
  52.6 4.3 %collective-permute-done.10 = f32[256,128]{1,0:T(8,128)S(1)} collective-permute-done((f32[256,128]{1,0:T(8,128)S(1)}, f32[256,128]{1,0:T(8,128)S(1)}, u32[]{:S(2)}, u32[]{:S(2)}) %collective-permute-start.10) | collective-permute-done | bytes 131104 | tf_op jit(solution)/shard_map/ppermute | solution.py:34
  57.3 1.0 collective-permute-start.5
  58.3 1.7 collective-permute-start.6
  61.4 2.5 %collective-permute-done.7.refs_5_ = f32[2,256,128]{2,1,0:T(8,128)} collective-permute-done((f32[2,256,128]{2,1,0:T(8,128)S(1)}, f32[2,256,128]{2,1,0:T(8,128)}, u32[]{:S(2)}, u32[]{:S(2)}) %collective-permute-start.7) | collective-permute-done | bytes 262176 | tf_op jit(solution)/shard_map/ppermute | solution.py:34
  65.1 2.2 collective-permute-start.15
  67.3 2.2 collective-permute-done.6.refs_4_
  70.3 2.2 collective-permute-start.25
  72.4 1.0 collective-permute-start.9
  75.3 2.2 collective-permute-start.18
  78.3 2.6 %collective-permute-done.8.refs_6_ = f32[2,256,128]{2,1,0:T(8,128)} collective-permute-done((f32[2,256,128]{2,1,0:T(8,128)}, f32[2,256,128]{2,1,0:T(8,128)}, u32[]{:S(2)}, u32[]{:S(2)}) %collective-permute-start.8) | collective-permute-done | bytes 262176 | tf_op jit(solution)/shard_map/ppermute | solution.py:34
  81.2 3.8 %collective-permute-done.17.refs_14_ = f32[2,256,128]{2,1,0:T(8,128)} collective-permute-done((f32[2,256,128]{2,1,0:T(8,128)}, f32[2,256,128]{2,1,0:T(8,128)}, u32[]{:S(2)}, u32[]{:S(2)}) %collective-permute-start.17) | collective-permute-done | bytes 262176 | tf_op jit(solution)/shard_map/ppermute | solution.py:34
  85.0 0.9 copy-done.3
  85.9 0.9 copy-done.5
  86.9 0.9 copy-done.7
  88.8 0.9 copy-done.11
  89.7 11.5 %pair_weights.1 = (f32[4,64,1024]{2,1,0:T(8,128)S(1)}, f32[4,64,1024]{2,1,0:T(8,128)S(1)}) custom-call(s32[4,16]{1,0:T(4,128)S(1)} %pad_add_fusion.order.refs_0_, s32[8]{0:T(128)S(1)} %fusion.24.panel_order, s32[5]{0:T(128)S(1)} %pad_add_fusion.1.chips.where, f32[2,256,128]{2,1,0:T(8,128)S(1)} %pad_maximum_fusion.refs_0_, ...), custom_call_target="tpu_custom_call" | custom-call | flops 6442450944 | bytes 12582912 | tf_op jit(solution)/shard_map/pair_weights/pallas_call | solution.py:177
  101.2 5.5 %collective-permute-start.26 = (f32[4,64,1024]{2,1,0:T(8,128)S(1)}, f32[4,64,1024]{2,1,0:T(8,128)S(1)}, u32[]{:S(2)}, u32[]{:S(2)}) collective-permute-start(f32[4,64,1024]{2,1,0:T(8,128)S(1)} %get-tuple-element.18), channel_id=1, source_target_pairs={{0,1},{1,0},{2,3},{3,2},{4,5},{5,4},{6,7},{7,6},{8,9},{9,8},{10,11... | collective-permute-start | bytes 3145736 | tf_op jit(solution)/shard_map/ppermute | solution.py:38
  106.8 2.3 collective-permute-done.26
  109.3 4.6 %collective-permute-start.28 = (f32[64,1024]{1,0:T(8,128)S(1)}, f32[64,1024]{1,0:T(8,128)S(1)}, u32[]{:S(2)}, u32[]{:S(2)}) collective-permute-start(f32[64,1024]{1,0:T(8,128)S(1)} %get-tuple-element.41), channel_id=1, source_target_pairs={{0,32},{1,120},{2,64},{3,88},{4,96},{5,56},{6,0},{7,24},{8,40},{9,... | collective-permute-start | bytes 786440 | tf_op jit(solution)/shard_map/ppermute | solution.py:56
  113.8 1.9 collective-permute-start.30
  115.8 4.7 %collective-permute-start.29 = (f32[64,1024]{1,0:T(8,128)S(1)}, f32[64,1024]{1,0:T(8,128)S(1)}, u32[]{:S(2)}, u32[]{:S(2)}) collective-permute-start(f32[64,1024]{1,0:T(8,128)S(1)} %get-tuple-element.43), channel_id=1, source_target_pairs={{0,64},{1,88},{2,96},{3,56},{4,0},{5,24},{6,32},{7,120},{8,72},{9,... | collective-permute-start | bytes 786440 | tf_op jit(solution)/shard_map/ppermute | solution.py:56
  120.5 3.9 %collective-permute-start.27 = (f32[64,1024]{1,0:T(8,128)S(1)}, f32[64,1024]{1,0:T(8,128)S(1)}, u32[]{:S(2)}, u32[]{:S(2)}) collective-permute-start(f32[64,1024]{1,0:T(8,128)S(1)} %get-tuple-element.44), channel_id=1, source_target_pairs={{0,0},{1,24},{2,32},{3,120},{4,64},{5,88},{6,96},{7,56},{8,8},{9,1... | collective-permute-start | bytes 786440 | tf_op jit(solution)/shard_map/ppermute | solution.py:56
  124.4 3.1 %collective-permute-done.29 = f32[64,1024]{1,0:T(8,128)S(1)} collective-permute-done((f32[64,1024]{1,0:T(8,128)S(1)}, f32[64,1024]{1,0:T(8,128)S(1)}, u32[]{:S(2)}, u32[]{:S(2)}) %collective-permute-start.29) | collective-permute-done | bytes 262176 | tf_op jit(solution)/shard_map/ppermute | solution.py:56
  127.5 1.6 collective-permute-done.27
  129.2 1.5 collective-permute-start.32
  131.4 4.0 %collective-permute-start.41 = (f32[32,1024]{1,0:T(8,128)S(1)}, f32[32,1024]{1,0:T(8,128)S(1)}, u32[]{:S(2)}, u32[]{:S(2)}) collective-permute-start(f32[32,1024]{1,0:T(8,128)S(1)} %get-tuple-element.47), channel_id=1, source_target_pairs={{0,96},{8,104},{16,112},{24,120},{32,0},{40,8},{48,16},{56,24},{64... | collective-permute-start | bytes 393224 | tf_op jit(solution)/shard_map/ppermute | solution.py:34
  135.4 10.1 %collective-permute-start.42 = (f32[32,1024]{1,0:T(8,128)S(1)}, f32[32,1024]{1,0:T(8,128)S(1)}, u32[]{:S(2)}, u32[]{:S(2)}) collective-permute-start(f32[32,1024]{1,0:T(8,128)S(1)} %get-tuple-element.47), channel_id=1, source_target_pairs={{0,64},{8,72},{16,80},{24,88},{32,96},{40,104},{48,112},{56,120},{... | collective-permute-start | bytes 393224 | tf_op jit(solution)/shard_map/ppermute | solution.py:34
  145.7 1.4 collective-permute-start.35
  147.2 1.4 collective-permute-start.36
  149.1 3.2 %collective-permute-start.46 = (f32[2,32,1024]{2,1,0:T(8,128)S(1)}, f32[2,32,1024]{2,1,0:T(8,128)S(1)}, u32[]{:S(2)}, u32[]{:S(2)}) collective-permute-start(f32[2,32,1024]{2,1,0:T(8,128)S(1)} %pad_maximum_fusion.7.refs_10_), channel_id=1, source_target_pairs={{0,24},{8,0},{16,8},{24,16},{32,56},{40,32},{48,40},{56,48},{64,88... | collective-permute-start | bytes 786440 | tf_op jit(solution)/shard_map/ppermute | solution.py:34
  152.5 1.0 collective-permute-done.35.refs_4_
  153.5 1.3 collective-permute-start.43
  154.8 3.0 %collective-permute-done.36.refs_5_ = f32[2,32,1024]{2,1,0:T(8,128)S(1)} collective-permute-done((f32[2,32,1024]{2,1,0:T(8,128)S(1)}, f32[2,32,1024]{2,1,0:T(8,128)S(1)}, u32[]{:S(2)}, u32[]{:S(2)}) %collective-permute-start.36) | collective-permute-done | bytes 262176 | tf_op jit(solution)/shard_map/ppermute | solution.py:34
  157.8 3.7 %collective-permute-start.45 = (f32[2,32,1024]{2,1,0:T(8,128)S(1)}, f32[2,32,1024]{2,1,0:T(8,128)S(1)}, u32[]{:S(2)}, u32[]{:S(2)}) collective-permute-start(f32[2,32,1024]{2,1,0:T(8,128)S(1)} %pad_maximum_fusion.6.refs_9_), channel_id=1, source_target_pairs={{0,24},{8,0},{16,8},{24,16},{32,56},{40,32},{48,40},{56,48},{64,88... | collective-permute-start | bytes 786440 | tf_op jit(solution)/shard_map/ppermute | solution.py:34
  161.6 1.5 collective-permute-start.39
  163.1 2.2 collective-permute-start.48
  165.4 1.8 collective-permute-done.39.refs_8_
  167.1 2.7 %collective-permute-done.38.refs_7_ = f32[2,32,1024]{2,1,0:T(8,128)S(1)} collective-permute-done((f32[2,32,1024]{2,1,0:T(8,128)S(1)}, f32[2,32,1024]{2,1,0:T(8,128)S(1)}, u32[]{:S(2)}, u32[]{:S(2)}) %collective-permute-start.38) | collective-permute-done | bytes 262176 | tf_op jit(solution)/shard_map/ppermute | solution.py:34
  169.8 1.6 collective-permute-done.48.refs_16_
  172.3 14.1 %term.2 = (f32[2,1024,128]{2,1,0:T(8,128)}, f32[2,1024,128]{2,1,0:T(8,128)}, f32[2,1024,128]{2,1,0:T(8,128)}, f32[2,1024,128]{2,1,0:T(8,128)}, bf16[1024,1024]{1,0:T(8,128)(2,1)}, /*index=5*/bf16[1024,1024]{1,0:T(8,128)(2,1)}) custom-call(s32[5]{0:T(128)} %copy-done.12, s32[4,16]{1,0:T(4,128)} %copy-done.1, f32[2,32,1024]{2,1,0:T(8,128)} %copy-done.19, ...), custom_call_target="tpu_custom_call" | custom-call | flops 6442450944 | bytes 16777216 | tf_op jit(solution)/shard_map/term/pallas_call | solution.py:287
  186.3 4.4 %collective-permute-start.49 = (f32[2,1024,128]{2,1,0:T(8,128)}, f32[2,1024,128]{2,1,0:T(8,128)S(1)}, u32[]{:S(2)}, u32[]{:S(2)}) collective-permute-start(f32[2,1024,128]{2,1,0:T(8,128)} %get-tuple-element.22), channel_id=1, source_target_pairs={{0,1},{1,0},{2,3},{3,2},{4,5},{5,4},{6,7},{7,6},{8,9},{9,8},{10,11... | collective-permute-start | bytes 3145736 | tf_op jit(solution)/shard_map/ppermute | solution.py:38
  190.8 2.4 collective-permute-done.49
  193.2 2.3 fusion.13
  195.5 11.7 %term.3 = (f32[2,1024,128]{2,1,0:T(8,128)}, f32[2,1024,128]{2,1,0:T(8,128)}, f32[2,1024,128]{2,1,0:T(8,128)}, f32[2,1024,128]{2,1,0:T(8,128)}) custom-call(s32[5]{0:T(128)} %copy-done.12, f32[2048,1024]{1,0:T(8,128)} %refs_0_.1, bf16[1024,1024]{1,0:T(8,128)(2,1)} %get-tuple-element.19.refs_1_.refs_3_, bf16[1024,1024]{1,0:T(8,128)(2,1)} %get-tuple-element.20.refs_2_.refs_4_, ...), custom_call_target="tpu_custom_call" | custom-call | flops 6442450944 | bytes 16777216 | tf_op jit(solution)/shard_map/term/pallas_call | solution.py:287
  207.9 2.7 %collective-permute-start.57 = (f32[1024,128]{1,0:T(8,128)S(1)}, f32[1024,128]{1,0:T(8,128)S(1)}, u32[]{:S(2)}, u32[]{:S(2)}) collective-permute-start(f32[1024,128]{1,0:T(8,128)S(1)} %get-tuple-element.38), channel_id=1, source_target_pairs={{0,6},{1,7},{2,0},{3,1},{4,2},{5,3},{6,4},{7,5},{8,14},{9,15},{10,... | collective-permute-start | bytes 1572872 | tf_op jit(solution)/shard_map/ppermute | solution.py:34
  211.3 11.2 %collective-permute-done.53 = f32[1024,128]{1,0:T(8,128)S(1)} collective-permute-done((f32[1024,128]{1,0:T(8,128)S(1)}, f32[1024,128]{1,0:T(8,128)S(1)}, u32[]{:S(2)}, u32[]{:S(2)}) %collective-permute-start.53) | collective-permute-done | bytes 524320 | tf_op jit(solution)/shard_map/ppermute | solution.py:34
  222.6 1.5 collective-permute-start.54
  224.1 1.2 collective-permute-start.58
  225.4 8.3 %collective-permute-done.56 = f32[1024,128]{1,0:T(8,128)S(1)} collective-permute-done((f32[1024,128]{1,0:T(8,128)S(1)}, f32[1024,128]{1,0:T(8,128)S(1)}, u32[]{:S(2)}, u32[]{:S(2)}) %collective-permute-start.56) | collective-permute-done | bytes 524320 | tf_op jit(solution)/shard_map/ppermute | solution.py:34
  234.3 10.6 %collective-permute-done.54 = f32[1024,128]{1,0:T(8,128)S(1)} collective-permute-done((f32[1024,128]{1,0:T(8,128)S(1)}, f32[1024,128]{1,0:T(8,128)S(1)}, u32[]{:S(2)}, u32[]{:S(2)}) %collective-permute-start.54) | collective-permute-done | bytes 524320 | tf_op jit(solution)/shard_map/ppermute | solution.py:34
  245.8 1.0 maximum_negate_fusion
  (185 shorter events, 16.2 us)
Async XLA Ops:
  5.8 18.0 %all-to-all-start = ((f32[16,64,128]{2,1,0:T(8,128)}), f32[16,64,128]{2,1,0:T(8,128)S(1)}, u32[]{:S(2)}, u32[]{:S(2)}) async-start(f32[16,64,128]{2,1,0:T(8,128)} %bitcast.2), calls=%async_computation | async-start | bytes 1048576 | tf_op jit(solution)/shard_map/all_to_all | solution.py:319
  23.8 46.4 %copy-start.35 = (s32[4]{0:T(128)S(1)}, s32[4]{0:T(128)}, u32[]{:S(2)}) copy-start(s32[4]{0:T(128)} %constant.140.clone) | copy-start | bytes 52
  24.9 8.4 %collective-permute-start = (f32[512,128]{1,0:T(8,128)S(1)}, f32[512,128]{1,0:T(8,128)S(1)}, u32[]{:S(2)}, u32[]{:S(2)}) collective-permute-start(f32[512,128]{1,0:T(8,128)S(1)} %gather_fusion.1), channel_id=1, source_target_pairs={{0,0},{1,24},{2,32},{3,120},{4,64},{5,88},{6,96},{7,56},{8,8},{9,1... | collective-permute-start | bytes 786440 | tf_op jit(solution)/shard_map/ppermute | solution.py:56
  29.1 11.4 %collective-permute-start.22 = (f32[1,512,128]{2,1,0:T(8,128)S(1)}, f32[1,512,128]{2,1,0:T(8,128)S(1)}, u32[]{:S(2)}, u32[]{:S(2)}) collective-permute-start(f32[1,512,128]{2,1,0:T(8,128)S(1)} %bitcast.65), channel_id=1, source_target_pairs={{0,6},{1,7},{2,0},{3,1},{4,2},{5,3},{6,4},{7,5},{8,14},{9,15},{10,... | collective-permute-start | bytes 786440 | tf_op jit(solution)/shard_map/ppermute | solution.py:34
  31.5 9.0 %collective-permute-start.20 = (f32[1,512,128]{2,1,0:T(8,128)S(1)}, f32[1,512,128]{2,1,0:T(8,128)S(1)}, u32[]{:S(2)}, u32[]{:S(2)}) collective-permute-start(f32[1,512,128]{2,1,0:T(8,128)S(1)} %bitcast.66), channel_id=1, source_target_pairs={{0,2},{1,3},{2,4},{3,5},{4,6},{5,7},{6,0},{7,1},{8,10},{9,11},{10,... | collective-permute-start | bytes 786440 | tf_op jit(solution)/shard_map/ppermute | solution.py:34
  31.7 19.2 %collective-permute-start.19 = (f32[1,512,128]{2,1,0:T(8,128)S(1)}, f32[1,512,128]{2,1,0:T(8,128)S(1)}, u32[]{:S(2)}, u32[]{:S(2)}) collective-permute-start(f32[1,512,128]{2,1,0:T(8,128)S(1)} %bitcast.67), channel_id=1, source_target_pairs={{0,1},{1,0},{2,3},{3,2},{4,5},{5,4},{6,7},{7,6},{8,9},{9,8},{10,11... | collective-permute-start | bytes 786440 | tf_op jit(solution)/shard_map/ppermute | solution.py:38
  33.3 8.7 %collective-permute-start.2 = (f32[256,128]{1,0:T(8,128)S(1)}, f32[256,128]{1,0:T(8,128)S(1)}, u32[]{:S(2)}, u32[]{:S(2)}) collective-permute-start(f32[256,128]{1,0:T(8,128)S(1)} %get-tuple-element.52), channel_id=1, source_target_pairs={{0,24},{8,0},{16,8},{24,16},{32,56},{40,32},{48,40},{56,48},{64,88... | collective-permute-start | bytes 393224 | tf_op jit(solution)/shard_map/ppermute | solution.py:34
  33.6 14.2 %collective-permute-start.1 = (f32[256,128]{1,0:T(8,128)S(1)}, f32[256,128]{1,0:T(8,128)S(1)}, u32[]{:S(2)}, u32[]{:S(2)}) collective-permute-start(f32[256,128]{1,0:T(8,128)S(1)} %get-tuple-element.52), channel_id=1, source_target_pairs={{0,8},{8,16},{16,24},{24,0},{32,40},{40,48},{48,56},{56,32},{64,72... | collective-permute-start | bytes 393224 | tf_op jit(solution)/shard_map/ppermute | solution.py:34
  40.5 7.4 %collective-permute-start.3 = (f32[256,128]{1,0:T(8,128)S(1)}, f32[256,128]{1,0:T(8,128)S(1)}, u32[]{:S(2)}, u32[]{:S(2)}) collective-permute-start(f32[256,128]{1,0:T(8,128)S(1)} %get-tuple-element.52), channel_id=1, source_target_pairs={{0,16},{8,24},{16,0},{24,8},{32,48},{40,56},{48,32},{56,40},{64,80... | collective-permute-start | bytes 393224 | tf_op jit(solution)/shard_map/ppermute | solution.py:34
  40.5 17.9 %collective-permute-start.24 = (f32[1,512,128]{2,1,0:T(8,128)S(1)}, f32[1,512,128]{2,1,0:T(8,128)S(1)}, u32[]{:S(2)}, u32[]{:S(2)}) collective-permute-start(f32[1,512,128]{2,1,0:T(8,128)S(1)} %collective-permute-done.20.refs_18_), channel_id=1, source_target_pairs={{0,2},{1,3},{2,4},{3,5},{4,6},{5,7},{6,0},{7,1},{8,10},{9,11},{10,... | collective-permute-start | bytes 786440 | tf_op jit(solution)/shard_map/ppermute | solution.py:34
  42.0 10.6 %collective-permute-start.11 = (f32[256,128]{1,0:T(8,128)S(1)}, f32[256,128]{1,0:T(8,128)S(1)}, u32[]{:S(2)}, u32[]{:S(2)}) collective-permute-start(f32[256,128]{1,0:T(8,128)S(1)} %get-tuple-element.51), channel_id=1, source_target_pairs={{0,96},{8,104},{16,112},{24,120},{32,0},{40,8},{48,16},{56,24},{64... | collective-permute-start | bytes 393224 | tf_op jit(solution)/shard_map/ppermute | solution.py:34
  47.8 9.0 %collective-permute-start.10 = (f32[256,128]{1,0:T(8,128)S(1)}, f32[256,128]{1,0:T(8,128)S(1)}, u32[]{:S(2)}, u32[]{:S(2)}) collective-permute-start(f32[256,128]{1,0:T(8,128)S(1)} %get-tuple-element.51), channel_id=1, source_target_pairs={{0,32},{8,40},{16,48},{24,56},{32,64},{40,72},{48,80},{56,88},{64,... | collective-permute-start | bytes 393224 | tf_op jit(solution)/shard_map/ppermute | solution.py:34
  47.8 9.5 %collective-permute-start.12 = (f32[256,128]{1,0:T(8,128)S(1)}, f32[256,128]{1,0:T(8,128)S(1)}, u32[]{:S(2)}, u32[]{:S(2)}) collective-permute-start(f32[256,128]{1,0:T(8,128)S(1)} %get-tuple-element.51), channel_id=1, source_target_pairs={{0,64},{8,72},{16,80},{24,88},{32,96},{40,104},{48,112},{56,120},{... | collective-permute-start | bytes 393224 | tf_op jit(solution)/shard_map/ppermute | solution.py:34
  51.0 9.1 %collective-permute-start.23 = (f32[1,512,128]{2,1,0:T(8,128)S(1)}, f32[1,512,128]{2,1,0:T(8,128)}, u32[]{:S(2)}, u32[]{:S(2)}) collective-permute-start(f32[1,512,128]{2,1,0:T(8,128)S(1)} %collective-permute-done.19.refs_17_), channel_id=1, source_target_pairs={{0,6},{1,7},{2,0},{3,1},{4,2},{5,3},{6,4},{7,5},{8,14},{9,15},{10,... | collective-permute-start | bytes 786440 | tf_op jit(solution)/shard_map/ppermute | solution.py:34
  52.6 7.6 %collective-permute-start.21 = (f32[1,512,128]{2,1,0:T(8,128)S(1)}, f32[1,512,128]{2,1,0:T(8,128)S(1)}, u32[]{:S(2)}, u32[]{:S(2)}) collective-permute-start(f32[1,512,128]{2,1,0:T(8,128)S(1)} %collective-permute-done.19.refs_17_), channel_id=1, source_target_pairs={{0,2},{1,3},{2,4},{3,5},{4,6},{5,7},{6,0},{7,1},{8,10},{9,11},{10,... | collective-permute-start | bytes 786440 | tf_op jit(solution)/shard_map/ppermute | solution.py:34
  56.9 7.1 %collective-permute-start.7 = (f32[2,256,128]{2,1,0:T(8,128)S(1)}, f32[2,256,128]{2,1,0:T(8,128)}, u32[]{:S(2)}, u32[]{:S(2)}) collective-permute-start(f32[2,256,128]{2,1,0:T(8,128)S(1)} %pad_maximum_fusion.1.refs_1_), channel_id=1, source_target_pairs={{0,96},{8,104},{16,112},{24,120},{32,0},{40,8},{48,16},{56,24},{64... | collective-permute-start | bytes 786440 | tf_op jit(solution)/shard_map/ppermute | solution.py:34
  57.3 7.0 %collective-permute-start.5 = (f32[2,256,128]{2,1,0:T(8,128)S(1)}, f32[2,256,128]{2,1,0:T(8,128)S(1)}, u32[]{:S(2)}, u32[]{:S(2)}) collective-permute-start(f32[2,256,128]{2,1,0:T(8,128)S(1)} %pad_maximum_fusion.1.refs_1_), channel_id=1, source_target_pairs={{0,32},{8,40},{16,48},{24,56},{32,64},{40,72},{48,80},{56,88},{64,... | collective-permute-start | bytes 786440 | tf_op jit(solution)/shard_map/ppermute | solution.py:34
  58.3 11.2 %collective-permute-start.6 = (f32[2,256,128]{2,1,0:T(8,128)S(1)}, f32[2,256,128]{2,1,0:T(8,128)S(1)}, u32[]{:S(2)}, u32[]{:S(2)}) collective-permute-start(f32[2,256,128]{2,1,0:T(8,128)S(1)} %pad_maximum_fusion.refs_0_), channel_id=1, source_target_pairs={{0,96},{8,104},{16,112},{24,120},{32,0},{40,8},{48,16},{56,24},{64... | collective-permute-start | bytes 786440 | tf_op jit(solution)/shard_map/ppermute | solution.py:34
  60.0 41.2 %copy-start.1 = (s32[4,16]{1,0:T(4,128)}, s32[4,16]{1,0:T(4,128)S(1)}, u32[]{:S(2)}) copy-start(s32[4,16]{1,0:T(4,128)S(1)} %pad_add_fusion.order.refs_0_) | copy-start | bytes 772
  60.1 10.2 %collective-permute-start.4 = (f32[2,256,128]{2,1,0:T(8,128)S(1)}, f32[2,256,128]{2,1,0:T(8,128)}, u32[]{:S(2)}, u32[]{:S(2)}) collective-permute-start(f32[2,256,128]{2,1,0:T(8,128)S(1)} %pad_maximum_fusion.refs_0_), channel_id=1, source_target_pairs={{0,32},{8,40},{16,48},{24,56},{32,64},{40,72},{48,80},{56,88},{64,... | collective-permute-start | bytes 786440 | tf_op jit(solution)/shard_map/ppermute | solution.py:34
  60.9 11.5 %collective-permute-start.16 = (f32[2,256,128]{2,1,0:T(8,128)S(1)}, f32[2,256,128]{2,1,0:T(8,128)}, u32[]{:S(2)}, u32[]{:S(2)}) collective-permute-start(f32[2,256,128]{2,1,0:T(8,128)S(1)} %pad_maximum_fusion.3.refs_9_), channel_id=1, source_target_pairs={{0,24},{8,0},{16,8},{24,16},{32,56},{40,32},{48,40},{56,48},{64,88... | collective-permute-start | bytes 786440 | tf_op jit(solution)/shard_map/ppermute | solution.py:34
  63.9 9.5 %collective-permute-start.14 = (f32[2,256,128]{2,1,0:T(8,128)S(1)}, f32[2,256,128]{2,1,0:T(8,128)S(1)}, u32[]{:S(2)}, u32[]{:S(2)}) collective-permute-start(f32[2,256,128]{2,1,0:T(8,128)S(1)} %pad_maximum_fusion.3.refs_9_), channel_id=1, source_target_pairs={{0,8},{8,16},{16,24},{24,0},{32,40},{40,48},{48,56},{56,32},{64,72... | collective-permute-start | bytes 786440 | tf_op jit(solution)/shard_map/ppermute | solution.py:34
  65.1 9.6 %collective-permute-start.15 = (f32[2,256,128]{2,1,0:T(8,128)S(1)}, f32[2,256,128]{2,1,0:T(8,128)S(1)}, u32[]{:S(2)}, u32[]{:S(2)}) collective-permute-start(f32[2,256,128]{2,1,0:T(8,128)S(1)} %pad_maximum_fusion.2.refs_8_), channel_id=1, source_target_pairs={{0,24},{8,0},{16,8},{24,16},{32,56},{40,32},{48,40},{56,48},{64,88... | collective-permute-start | bytes 786440 | tf_op jit(solution)/shard_map/ppermute | solution.py:34
  70.2 7.7 %collective-permute-start.13 = (f32[2,256,128]{2,1,0:T(8,128)S(1)}, f32[2,256,128]{2,1,0:T(8,128)}, u32[]{:S(2)}, u32[]{:S(2)}) collective-permute-start(f32[2,256,128]{2,1,0:T(8,128)S(1)} %pad_maximum_fusion.2.refs_8_), channel_id=1, source_target_pairs={{0,8},{8,16},{16,24},{24,0},{32,40},{40,48},{48,56},{56,32},{64,72... | collective-permute-start | bytes 786440 | tf_op jit(solution)/shard_map/ppermute | solution.py:34
  70.3 8.0 %collective-permute-start.25 = (f32[1,512,128]{2,1,0:T(8,128)}, f32[1,512,128]{2,1,0:T(8,128)}, u32[]{:S(2)}, u32[]{:S(2)}) collective-permute-start(f32[1,512,128]{2,1,0:T(8,128)} %collective-permute-done.23.refs_21_), channel_id=1, source_target_pairs={{0,6},{1,7},{2,0},{3,1},{4,2},{5,3},{6,4},{7,5},{8,14},{9,15},{10,... | collective-permute-start | bytes 786440 | tf_op jit(solution)/shard_map/ppermute | solution.py:34
  72.4 5.8 %collective-permute-start.9 = (f32[2,256,128]{2,1,0:T(8,128)}, f32[2,256,128]{2,1,0:T(8,128)}, u32[]{:S(2)}, u32[]{:S(2)}) collective-permute-start(f32[2,256,128]{2,1,0:T(8,128)} %collective-permute-done.7.refs_5_), channel_id=1, source_target_pairs={{0,96},{8,104},{16,112},{24,120},{32,0},{40,8},{48,16},{56,24},{64... | collective-permute-start | bytes 786440 | tf_op jit(solution)/shard_map/ppermute | solution.py:34
  74.1 6.7 %collective-permute-start.8 = (f32[2,256,128]{2,1,0:T(8,128)}, f32[2,256,128]{2,1,0:T(8,128)}, u32[]{:S(2)}, u32[]{:S(2)}) collective-permute-start(f32[2,256,128]{2,1,0:T(8,128)} %collective-permute-done.4.refs_2_), channel_id=1, source_target_pairs={{0,32},{8,40},{16,48},{24,56},{32,64},{40,72},{48,80},{56,88},{64,... | collective-permute-start | bytes 786440 | tf_op jit(solution)/shard_map/ppermute | solution.py:34
  75.3 5.8 %collective-permute-start.18 = (f32[2,256,128]{2,1,0:T(8,128)}, f32[2,256,128]{2,1,0:T(8,128)}, u32[]{:S(2)}, u32[]{:S(2)}) collective-permute-start(f32[2,256,128]{2,1,0:T(8,128)} %collective-permute-done.16.refs_13_), channel_id=1, source_target_pairs={{0,24},{8,0},{16,8},{24,16},{32,56},{40,32},{48,40},{56,48},{64,88... | collective-permute-start | bytes 786440 | tf_op jit(solution)/shard_map/ppermute | solution.py:34
  77.9 7.0 %collective-permute-start.17 = (f32[2,256,128]{2,1,0:T(8,128)}, f32[2,256,128]{2,1,0:T(8,128)}, u32[]{:S(2)}, u32[]{:S(2)}) collective-permute-start(f32[2,256,128]{2,1,0:T(8,128)} %collective-permute-done.13.refs_10_), channel_id=1, source_target_pairs={{0,8},{8,16},{16,24},{24,0},{32,40},{40,48},{48,56},{56,32},{64,72... | collective-permute-start | bytes 786440 | tf_op jit(solution)/shard_map/ppermute | solution.py:34
  101.2 7.8 %collective-permute-start.26 = (f32[4,64,1024]{2,1,0:T(8,128)S(1)}, f32[4,64,1024]{2,1,0:T(8,128)S(1)}, u32[]{:S(2)}, u32[]{:S(2)}) collective-permute-start(f32[4,64,1024]{2,1,0:T(8,128)S(1)} %get-tuple-element.18), channel_id=1, source_target_pairs={{0,1},{1,0},{2,3},{3,2},{4,5},{5,4},{6,7},{7,6},{8,9},{9,8},{10,11... | collective-permute-start | bytes 3145736 | tf_op jit(solution)/shard_map/ppermute | solution.py:38
  109.3 15.1 %collective-permute-start.28 = (f32[64,1024]{1,0:T(8,128)S(1)}, f32[64,1024]{1,0:T(8,128)S(1)}, u32[]{:S(2)}, u32[]{:S(2)}) collective-permute-start(f32[64,1024]{1,0:T(8,128)S(1)} %get-tuple-element.41), channel_id=1, source_target_pairs={{0,32},{1,120},{2,64},{3,88},{4,96},{5,56},{6,0},{7,24},{8,40},{9,... | collective-permute-start | bytes 786440 | tf_op jit(solution)/shard_map/ppermute | solution.py:56
  113.8 10.5 %collective-permute-start.30 = (f32[64,1024]{1,0:T(8,128)S(1)}, f32[64,1024]{1,0:T(8,128)S(1)}, u32[]{:S(2)}, u32[]{:S(2)}) collective-permute-start(f32[64,1024]{1,0:T(8,128)S(1)} %get-tuple-element.42), channel_id=1, source_target_pairs={{0,96},{1,56},{2,0},{3,24},{4,32},{5,120},{6,64},{7,88},{8,104},{9... | collective-permute-start | bytes 786440 | tf_op jit(solution)/shard_map/ppermute | solution.py:56
  115.8 11.8 %collective-permute-start.29 = (f32[64,1024]{1,0:T(8,128)S(1)}, f32[64,1024]{1,0:T(8,128)S(1)}, u32[]{:S(2)}, u32[]{:S(2)}) collective-permute-start(f32[64,1024]{1,0:T(8,128)S(1)} %get-tuple-element.43), channel_id=1, source_target_pairs={{0,64},{1,88},{2,96},{3,56},{4,0},{5,24},{6,32},{7,120},{8,72},{9,... | collective-permute-start | bytes 786440 | tf_op jit(solution)/shard_map/ppermute | solution.py:56
  120.5 8.6 %collective-permute-start.27 = (f32[64,1024]{1,0:T(8,128)S(1)}, f32[64,1024]{1,0:T(8,128)S(1)}, u32[]{:S(2)}, u32[]{:S(2)}) collective-permute-start(f32[64,1024]{1,0:T(8,128)S(1)} %get-tuple-element.44), channel_id=1, source_target_pairs={{0,0},{1,24},{2,32},{3,120},{4,64},{5,88},{6,96},{7,56},{8,8},{9,1... | collective-permute-start | bytes 786440 | tf_op jit(solution)/shard_map/ppermute | solution.py:56
  129.2 6.2 %collective-permute-start.32 = (f32[32,1024]{1,0:T(8,128)S(1)}, f32[32,1024]{1,0:T(8,128)S(1)}, u32[]{:S(2)}, u32[]{:S(2)}) collective-permute-start(f32[32,1024]{1,0:T(8,128)S(1)} %get-tuple-element.48), channel_id=1, source_target_pairs={{0,24},{8,0},{16,8},{24,16},{32,56},{40,32},{48,40},{56,48},{64,88... | collective-permute-start | bytes 393224 | tf_op jit(solution)/shard_map/ppermute | solution.py:34
  130.7 14.8 %collective-permute-start.33 = (f32[32,1024]{1,0:T(8,128)S(1)}, f32[32,1024]{1,0:T(8,128)S(1)}, u32[]{:S(2)}, u32[]{:S(2)}) collective-permute-start(f32[32,1024]{1,0:T(8,128)S(1)} %get-tuple-element.48), channel_id=1, source_target_pairs={{0,16},{8,24},{16,0},{24,8},{32,48},{40,56},{48,32},{56,40},{64,80... | collective-permute-start | bytes 393224 | tf_op jit(solution)/shard_map/ppermute | solution.py:34
  130.7 15.0 %collective-permute-start.31 = (f32[32,1024]{1,0:T(8,128)S(1)}, f32[32,1024]{1,0:T(8,128)S(1)}, u32[]{:S(2)}, u32[]{:S(2)}) collective-permute-start(f32[32,1024]{1,0:T(8,128)S(1)} %get-tuple-element.48), channel_id=1, source_target_pairs={{0,8},{8,16},{16,24},{24,0},{32,40},{40,48},{48,56},{56,32},{64,72... | collective-permute-start | bytes 393224 | tf_op jit(solution)/shard_map/ppermute | solution.py:34
  131.4 15.8 %collective-permute-start.41 = (f32[32,1024]{1,0:T(8,128)S(1)}, f32[32,1024]{1,0:T(8,128)S(1)}, u32[]{:S(2)}, u32[]{:S(2)}) collective-permute-start(f32[32,1024]{1,0:T(8,128)S(1)} %get-tuple-element.47), channel_id=1, source_target_pairs={{0,96},{8,104},{16,112},{24,120},{32,0},{40,8},{48,16},{56,24},{64... | collective-permute-start | bytes 393224 | tf_op jit(solution)/shard_map/ppermute | solution.py:34
  135.4 13.7 %collective-permute-start.40 = (f32[32,1024]{1,0:T(8,128)S(1)}, f32[32,1024]{1,0:T(8,128)S(1)}, u32[]{:S(2)}, u32[]{:S(2)}) collective-permute-start(f32[32,1024]{1,0:T(8,128)S(1)} %get-tuple-element.47), channel_id=1, source_target_pairs={{0,32},{8,40},{16,48},{24,56},{32,64},{40,72},{48,80},{56,88},{64,... | collective-permute-start | bytes 393224 | tf_op jit(solution)/shard_map/ppermute | solution.py:34
  135.4 13.1 %collective-permute-start.42 = (f32[32,1024]{1,0:T(8,128)S(1)}, f32[32,1024]{1,0:T(8,128)S(1)}, u32[]{:S(2)}, u32[]{:S(2)}) collective-permute-start(f32[32,1024]{1,0:T(8,128)S(1)} %get-tuple-element.47), channel_id=1, source_target_pairs={{0,64},{8,72},{16,80},{24,88},{32,96},{40,104},{48,112},{56,120},{... | collective-permute-start | bytes 393224 | tf_op jit(solution)/shard_map/ppermute | solution.py:34
  145.6 26.6 %copy-start.18 = (f32[2,32,1024]{2,1,0:T(8,128)}, f32[2,32,1024]{2,1,0:T(8,128)S(1)}, u32[]{:S(2)}) copy-start(f32[2,32,1024]{2,1,0:T(8,128)S(1)} %pad_maximum_fusion.5.refs_2_) | copy-start | bytes 786436
  145.6 6.8 %collective-permute-start.37 = (f32[2,32,1024]{2,1,0:T(8,128)S(1)}, f32[2,32,1024]{2,1,0:T(8,128)S(1)}, u32[]{:S(2)}, u32[]{:S(2)}) collective-permute-start(f32[2,32,1024]{2,1,0:T(8,128)S(1)} %pad_maximum_fusion.5.refs_2_), channel_id=1, source_target_pairs={{0,96},{8,104},{16,112},{24,120},{32,0},{40,8},{48,16},{56,24},{64... | collective-permute-start | bytes 786440 | tf_op jit(solution)/shard_map/ppermute | solution.py:34
  145.7 7.8 %collective-permute-start.35 = (f32[2,32,1024]{2,1,0:T(8,128)S(1)}, f32[2,32,1024]{2,1,0:T(8,128)S(1)}, u32[]{:S(2)}, u32[]{:S(2)}) collective-permute-start(f32[2,32,1024]{2,1,0:T(8,128)S(1)} %pad_maximum_fusion.5.refs_2_), channel_id=1, source_target_pairs={{0,32},{8,40},{16,48},{24,56},{32,64},{40,72},{48,80},{56,88},{64,... | collective-permute-start | bytes 786440 | tf_op jit(solution)/shard_map/ppermute | solution.py:34
  147.2 25.0 %copy-start.19 = (f32[2,32,1024]{2,1,0:T(8,128)}, f32[2,32,1024]{2,1,0:T(8,128)S(1)}, u32[]{:S(2)}) copy-start(f32[2,32,1024]{2,1,0:T(8,128)S(1)} %pad_maximum_fusion.4.refs_1_) | copy-start | bytes 786436
  147.2 10.6 %collective-permute-start.36 = (f32[2,32,1024]{2,1,0:T(8,128)S(1)}, f32[2,32,1024]{2,1,0:T(8,128)S(1)}, u32[]{:S(2)}, u32[]{:S(2)}) collective-permute-start(f32[2,32,1024]{2,1,0:T(8,128)S(1)} %pad_maximum_fusion.4.refs_1_), channel_id=1, source_target_pairs={{0,96},{8,104},{16,112},{24,120},{32,0},{40,8},{48,16},{56,24},{64... | collective-permute-start | bytes 786440 | tf_op jit(solution)/shard_map/ppermute | solution.py:34
  148.6 13.0 %collective-permute-start.34 = (f32[2,32,1024]{2,1,0:T(8,128)S(1)}, f32[2,32,1024]{2,1,0:T(8,128)S(1)}, u32[]{:S(2)}, u32[]{:S(2)}) collective-permute-start(f32[2,32,1024]{2,1,0:T(8,128)S(1)} %pad_maximum_fusion.4.refs_1_), channel_id=1, source_target_pairs={{0,32},{8,40},{16,48},{24,56},{32,64},{40,72},{48,80},{56,88},{64,... | collective-permute-start | bytes 786440 | tf_op jit(solution)/shard_map/ppermute | solution.py:34
  149.1 13.9 %collective-permute-start.46 = (f32[2,32,1024]{2,1,0:T(8,128)S(1)}, f32[2,32,1024]{2,1,0:T(8,128)S(1)}, u32[]{:S(2)}, u32[]{:S(2)}) collective-permute-start(f32[2,32,1024]{2,1,0:T(8,128)S(1)} %pad_maximum_fusion.7.refs_10_), channel_id=1, source_target_pairs={{0,24},{8,0},{16,8},{24,16},{32,56},{40,32},{48,40},{56,48},{64,88... | collective-permute-start | bytes 786440 | tf_op jit(solution)/shard_map/ppermute | solution.py:34
  152.4 10.6 %collective-permute-start.44 = (f32[2,32,1024]{2,1,0:T(8,128)S(1)}, f32[2,32,1024]{2,1,0:T(8,128)S(1)}, u32[]{:S(2)}, u32[]{:S(2)}) collective-permute-start(f32[2,32,1024]{2,1,0:T(8,128)S(1)} %pad_maximum_fusion.7.refs_10_), channel_id=1, source_target_pairs={{0,8},{8,16},{16,24},{24,0},{32,40},{40,48},{48,56},{56,32},{64,72... | collective-permute-start | bytes 786440 | tf_op jit(solution)/shard_map/ppermute | solution.py:34
  153.5 11.8 %collective-permute-start.43 = (f32[2,32,1024]{2,1,0:T(8,128)S(1)}, f32[2,32,1024]{2,1,0:T(8,128)S(1)}, u32[]{:S(2)}, u32[]{:S(2)}) collective-permute-start(f32[2,32,1024]{2,1,0:T(8,128)S(1)} %pad_maximum_fusion.6.refs_9_), channel_id=1, source_target_pairs={{0,8},{8,16},{16,24},{24,0},{32,40},{40,48},{48,56},{56,32},{64,72... | collective-permute-start | bytes 786440 | tf_op jit(solution)/shard_map/ppermute | solution.py:34
  157.8 7.5 %collective-permute-start.45 = (f32[2,32,1024]{2,1,0:T(8,128)S(1)}, f32[2,32,1024]{2,1,0:T(8,128)S(1)}, u32[]{:S(2)}, u32[]{:S(2)}) collective-permute-start(f32[2,32,1024]{2,1,0:T(8,128)S(1)} %pad_maximum_fusion.6.refs_9_), channel_id=1, source_target_pairs={{0,24},{8,0},{16,8},{24,16},{32,56},{40,32},{48,40},{56,48},{64,88... | collective-permute-start | bytes 786440 | tf_op jit(solution)/shard_map/ppermute | solution.py:34
  161.6 5.6 %collective-permute-start.39 = (f32[2,32,1024]{2,1,0:T(8,128)S(1)}, f32[2,32,1024]{2,1,0:T(8,128)S(1)}, u32[]{:S(2)}, u32[]{:S(2)}) collective-permute-start(f32[2,32,1024]{2,1,0:T(8,128)S(1)} %collective-permute-done.37.refs_6_), channel_id=1, source_target_pairs={{0,96},{8,104},{16,112},{24,120},{32,0},{40,8},{48,16},{56,24},{64... | collective-permute-start | bytes 786440 | tf_op jit(solution)/shard_map/ppermute | solution.py:34
  163.1 6.8 %collective-permute-start.38 = (f32[2,32,1024]{2,1,0:T(8,128)S(1)}, f32[2,32,1024]{2,1,0:T(8,128)S(1)}, u32[]{:S(2)}, u32[]{:S(2)}) collective-permute-start(f32[2,32,1024]{2,1,0:T(8,128)S(1)} %collective-permute-done.34.refs_3_), channel_id=1, source_target_pairs={{0,32},{8,40},{16,48},{24,56},{32,64},{40,72},{48,80},{56,88},{64,... | collective-permute-start | bytes 786440 | tf_op jit(solution)/shard_map/ppermute | solution.py:34
  163.1 8.4 %collective-permute-start.48 = (f32[2,32,1024]{2,1,0:T(8,128)S(1)}, f32[2,32,1024]{2,1,0:T(8,128)S(1)}, u32[]{:S(2)}, u32[]{:S(2)}) collective-permute-start(f32[2,32,1024]{2,1,0:T(8,128)S(1)} %collective-permute-done.46.refs_14_), channel_id=1, source_target_pairs={{0,24},{8,0},{16,8},{24,16},{32,56},{40,32},{48,40},{56,48},{64,88... | collective-permute-start | bytes 786440 | tf_op jit(solution)/shard_map/ppermute | solution.py:34
  165.3 6.9 %collective-permute-start.47 = (f32[2,32,1024]{2,1,0:T(8,128)S(1)}, f32[2,32,1024]{2,1,0:T(8,128)}, u32[]{:S(2)}, u32[]{:S(2)}) collective-permute-start(f32[2,32,1024]{2,1,0:T(8,128)S(1)} %collective-permute-done.43.refs_11_), channel_id=1, source_target_pairs={{0,8},{8,16},{16,24},{24,0},{32,40},{40,48},{48,56},{56,32},{64,72... | collective-permute-start | bytes 786440 | tf_op jit(solution)/shard_map/ppermute | solution.py:34
  186.3 6.9 %collective-permute-start.49 = (f32[2,1024,128]{2,1,0:T(8,128)}, f32[2,1024,128]{2,1,0:T(8,128)S(1)}, u32[]{:S(2)}, u32[]{:S(2)}) collective-permute-start(f32[2,1024,128]{2,1,0:T(8,128)} %get-tuple-element.22), channel_id=1, source_target_pairs={{0,1},{1,0},{2,3},{3,2},{4,5},{5,4},{6,7},{7,6},{8,9},{9,8},{10,11... | collective-permute-start | bytes 3145736 | tf_op jit(solution)/shard_map/ppermute | solution.py:38
  190.7 17.0 %collective-permute-start.52 = (f32[2,1024,128]{2,1,0:T(8,128)}, f32[2,1024,128]{2,1,0:T(8,128)S(1)}, u32[]{:S(2)}, u32[]{:S(2)}) collective-permute-start(f32[2,1024,128]{2,1,0:T(8,128)} %get-tuple-element.28), channel_id=1, source_target_pairs={{0,1},{1,0},{2,3},{3,2},{4,5},{5,4},{6,7},{7,6},{8,9},{9,8},{10,11... | collective-permute-start | bytes 3145736 | tf_op jit(solution)/shard_map/ppermute | solution.py:38
  207.2 15.2 %collective-permute-start.51 = (f32[2,1024,128]{2,1,0:T(8,128)}, f32[2,1024,128]{2,1,0:T(8,128)S(1)}, u32[]{:S(2)}, u32[]{:S(2)}) collective-permute-start(f32[2,1024,128]{2,1,0:T(8,128)} %get-tuple-element.26), channel_id=1, source_target_pairs={{0,1},{1,0},{2,3},{3,2},{4,5},{5,4},{6,7},{7,6},{8,9},{9,8},{10,11... | collective-permute-start | bytes 3145736 | tf_op jit(solution)/shard_map/ppermute | solution.py:38
  207.8 14.6 %collective-permute-start.53 = (f32[1024,128]{1,0:T(8,128)S(1)}, f32[1024,128]{1,0:T(8,128)S(1)}, u32[]{:S(2)}, u32[]{:S(2)}) collective-permute-start(f32[1024,128]{1,0:T(8,128)S(1)} %get-tuple-element.37), channel_id=1, source_target_pairs={{0,2},{1,3},{2,4},{3,5},{4,6},{5,7},{6,0},{7,1},{8,10},{9,11},{10,... | collective-permute-start | bytes 1572872 | tf_op jit(solution)/shard_map/ppermute | solution.py:34
  207.9 14.5 %collective-permute-start.57 = (f32[1024,128]{1,0:T(8,128)S(1)}, f32[1024,128]{1,0:T(8,128)S(1)}, u32[]{:S(2)}, u32[]{:S(2)}) collective-permute-start(f32[1024,128]{1,0:T(8,128)S(1)} %get-tuple-element.38), channel_id=1, source_target_pairs={{0,6},{1,7},{2,0},{3,1},{4,2},{5,3},{6,4},{7,5},{8,14},{9,15},{10,... | collective-permute-start | bytes 1572872 | tf_op jit(solution)/shard_map/ppermute | solution.py:34
  210.6 23.8 %collective-permute-start.50 = (f32[2,1024,128]{2,1,0:T(8,128)S(1)}, f32[2,1024,128]{2,1,0:T(8,128)S(1)}, u32[]{:S(2)}, u32[]{:S(2)}) collective-permute-start(f32[2,1024,128]{2,1,0:T(8,128)S(1)} %copy-done.23), channel_id=1, source_target_pairs={{0,1},{1,0},{2,3},{3,2},{4,5},{5,4},{6,7},{7,6},{8,9},{9,8},{10,11... | collective-permute-start | bytes 3145736 | tf_op jit(solution)/shard_map/ppermute | solution.py:38
  211.3 22.4 %collective-permute-start.56 = (f32[1024,128]{1,0:T(8,128)S(1)}, f32[1024,128]{1,0:T(8,128)S(1)}, u32[]{:S(2)}, u32[]{:S(2)}) collective-permute-start(f32[1024,128]{1,0:T(8,128)S(1)} %copy-done.17), channel_id=1, source_target_pairs={{0,2},{1,3},{2,4},{3,5},{4,6},{5,7},{6,0},{7,1},{8,10},{9,11},{10,... | collective-permute-start | bytes 1572872 | tf_op jit(solution)/shard_map/ppermute | solution.py:34
  222.4 11.9 %collective-permute-start.55 = (f32[1024,128]{1,0:T(8,128)S(1)}, f32[1024,128]{1,0:T(8,128)S(1)}, u32[]{:S(2)}, u32[]{:S(2)}) collective-permute-start(f32[1024,128]{1,0:T(8,128)S(1)} %copy-done.16), channel_id=1, source_target_pairs={{0,6},{1,7},{2,0},{3,1},{4,2},{5,3},{6,4},{7,5},{8,14},{9,15},{10,... | collective-permute-start | bytes 1572872 | tf_op jit(solution)/shard_map/ppermute | solution.py:34
  222.6 22.3 %collective-permute-start.54 = (f32[1024,128]{1,0:T(8,128)S(1)}, f32[1024,128]{1,0:T(8,128)S(1)}, u32[]{:S(2)}, u32[]{:S(2)}) collective-permute-start(f32[1024,128]{1,0:T(8,128)S(1)} %get-tuple-element.35), channel_id=1, source_target_pairs={{0,2},{1,3},{2,4},{3,5},{4,6},{5,7},{6,0},{7,1},{8,10},{9,11},{10,... | collective-permute-start | bytes 1572872 | tf_op jit(solution)/shard_map/ppermute | solution.py:34
  224.1 21.4 %collective-permute-start.58 = (f32[1024,128]{1,0:T(8,128)S(1)}, f32[1024,128]{1,0:T(8,128)S(1)}, u32[]{:S(2)}, u32[]{:S(2)}) collective-permute-start(f32[1024,128]{1,0:T(8,128)S(1)} %get-tuple-element.36), channel_id=1, source_target_pairs={{0,6},{1,7},{2,0},{3,1},{4,2},{5,3},{6,4},{7,5},{8,14},{9,15},{10,... | collective-permute-start | bytes 1572872 | tf_op jit(solution)/shard_map/ppermute | solution.py:34
  (32 other events, 261.1 us)
where the time goes:
time: 249 us; the launch traced here: 247 us
  starting transfers between devices  104 us (42%)
  waiting for transfers between devices  83.1 us (33%)
  Pallas kernels  37.3 us (15%)
  local copies, waits for them, and re-layouts  15.1 us (6%)
  other arithmetic  5.71 us (2%)
    ppermute x48, starting transfers between devices, move(): return lax.ppermute(value, name, pairs)  65 us
    ppermute x48, waiting for transfers between devices, move(): return lax.ppermute(value, name, pairs)  63.7 us
    pallas_call x2, Pallas kernels, term(): pl.pallas_call(functools.partial(term_kernel, gathered is not None), out_...  25.8 us
    ppermute x5, starting transfers between devices, to_plane(): return lax.ppermute(value, ('row', 'col'), scatter_pairs(turn))  19.2 us
    ppermute x6, starting transfers between devices, swap_cores(): return lax.ppermute(value, 'col', [(c, c ^ 1) for c in range(2 * SIDE)])  12.7 us
    pallas_call x1, Pallas kernels, pair_weights(): pl.pallas_call(pair_kernel, out_shape=(out, out), in_specs=[scalars, scal...  11.5 us
    all_to_all x1, waiting for transfers between devices, picked_strip(): lax.all_to_all(outgoing, 'row', split_axis=0, concat_axis=0, tiled=True)  9.94 us
    unnamed x72, local copies, waits for them, and re-layouts  9.07 us
  transfers between devices with their start and end apart: 60, of which 24 were waited for; matrix products, arithmetic and copies ran while one was open for 2% of the time, Pallas kernels for 5%

commit v1 on v0

--- a/solution.py
+++ b/solution.py
@@ -45,7 +45,7 @@
             for z in range(SIDE):
                 for k in range(2):
                     strip = (z + turn) % SIDE
-                    ty = ((strip if k == 0 else -strip) - y) % SIDE
+                    ty = (strip - y) % SIDE
                     tx = x if k == 0 else x ^ 3
                     target = (ty * SIDE + tx) * 8 + y * 2 + (x >> 1)
                     pairs.append(((y * SIDE + x) * 8 + z * 2 + k, target))
@@ -85,7 +85,7 @@
         py, px = (y + dy) % SIDE, (x + dx) % SIDE
         strip_k = (px >> 1) ^ k
         panel = (px & 1) ^ strip_k
-        return panel, (jnp.where(strip_k == 0, py + z, -py - z) % SIDE) * 2 + strip_k
+        return panel, ((py + z) % SIDE) * 2 + strip_k
 
     first, second = describe(outer, inner), describe(inner, outer)
     return jnp.stack([first[0], first[1], second[0], second[1]])
@@ -282,7 +282,7 @@
                 (points, bands // SIDE), lambda i, where, group=group: (0, chip_of(False, group, i, where))
             )
             in_specs += [chosen, chosen]
-        in_specs += [anywhere] * 2
+        in_specs += [pl.BlockSpec(memory_space=pl.ANY)] * 2
         operands = (fitting, *weights, *weights, *after)
     return pl.pallas_call(
         functools.partial(term_kernel, gathered is not None),

time: 249 us -> 248 us (level)
    ppermute x48, starting transfers between devices: 65 us -> 68.9 us  [move(): return lax.ppermute(value, name, pairs)]
    ppermute x48, waiting for transfers between devices: 63.7 us -> 60.6 us  [move(): return lax.ppermute(value, name, pairs)]
  transfers between devices with their start and end apart: 60 -> 60, of which waited for: 24 -> 26; matrix products, arithmetic and copies ran while one was open for 2% -> 2% of each run, Pallas kernels for 5% -> 5%
where the time goes in v1:
time: 248 us; the launch traced here: 247 us
  starting transfers between devices  106 us (43%)
  waiting for transfers between devices  80.9 us (33%)
  Pallas kernels  37.3 us (15%)
  local copies, waits for them, and re-layouts  15.1 us (6%)
  other arithmetic  5.7 us (2%)
    ppermute x48, starting transfers between devices, move(): return lax.ppermute(value, name, pairs)  68.9 us
    ppermute x48, waiting for transfers between devices, move(): return lax.ppermute(value, name, pairs)  60.6 us
    pallas_call x2, Pallas kernels, term(): pl.pallas_call(functools.partial(term_kernel, gathered is not None), out_...  25.8 us
    ppermute x5, starting transfers between devices, to_plane(): return lax.ppermute(value, ('row', 'col'), scatter_pairs(turn))  17.6 us
    ppermute x6, starting transfers between devices, swap_cores(): return lax.ppermute(value, 'col', [(c, c ^ 1) for c in range(2 * SIDE)])  12.4 us
    pallas_call x1, Pallas kernels, pair_weights(): pl.pallas_call(pair_kernel, out_shape=(out, out), in_specs=[scalars, scal...  11.5 us
    all_to_all x1, waiting for transfers between devices, picked_strip(): lax.all_to_all(outgoing, 'row', split_axis=0, concat_axis=0, tiled=True)  9.94 us
    unnamed x72, local copies, waits for them, and re-layouts  9.08 us
  transfers between devices with their start and end apart: 60, of which 26 were waited for; matrix products, arithmetic and copies ran while one was open for 2% of the time, Pallas kernels for 5%

profile of v1, /device:TPU:1, one launch (start us, length us, event | category | flops | bytes accessed | tf_op | source)
XLA Modules:
  0.0 246.6 jit_solution(9642890377587378737)
XLA Ops:
  1.8 4.0 %gather_fusion = f32[1024,128]{1,0:T(8,128)} fusion(f32[2048,128]{1,0:T(8,128)S(1)} %copy-done, s32[1024]{0:T(1024)S(1)} %broadcast_clamp_fusion), kind=kCustom, calls=%fused_computation | custom fusion | bytes 1052672 | tf_op jit(solution)/shard_map/gather | solution.py:318
  5.8 7.6 %all-to-all-start = ((f32[16,64,128]{2,1,0:T(8,128)}), f32[16,64,128]{2,1,0:T(8,128)S(1)}, u32[]{:S(2)}, u32[]{:S(2)}) async-start(f32[16,64,128]{2,1,0:T(8,128)} %bitcast.2), calls=%async_computation | async-start | bytes 1048576 | tf_op jit(solution)/shard_map/all_to_all | solution.py:319
  13.9 9.9 %all-to-all-done = f32[16,64,128]{2,1,0:T(8,128)S(1)} async-done(((f32[16,64,128]{2,1,0:T(8,128)}), f32[16,64,128]{2,1,0:T(8,128)S(1)}, u32[]{:S(2)}, u32[]{:S(2)}) %all-to-all-start) | async-done | bytes 524320 | tf_op jit(solution)/shard_map/all_to_all | solution.py:319
  23.8 1.0 gather_fusion.1
  24.9 4.1 %collective-permute-start = (f32[512,128]{1,0:T(8,128)S(1)}, f32[512,128]{1,0:T(8,128)S(1)}, u32[]{:S(2)}, u32[]{:S(2)}) collective-permute-start(f32[512,128]{1,0:T(8,128)S(1)} %gather_fusion.1), channel_id=1, source_target_pairs={{0,0},{1,24},{2,32},{3,56},{4,64},{5,88},{6,96},{7,120},{8,8},{9,1... | collective-permute-start | bytes 786440 | tf_op jit(solution)/shard_map/ppermute | solution.py:56
  29.1 3.0 %collective-permute-start.22 = (f32[1,512,128]{2,1,0:T(8,128)S(1)}, f32[1,512,128]{2,1,0:T(8,128)S(1)}, u32[]{:S(2)}, u32[]{:S(2)}) collective-permute-start(f32[1,512,128]{2,1,0:T(8,128)S(1)} %bitcast.65), channel_id=1, source_target_pairs={{0,6},{1,7},{2,0},{3,1},{4,2},{5,3},{6,4},{7,5},{8,14},{9,15},{10,... | collective-permute-start | bytes 786440 | tf_op jit(solution)/shard_map/ppermute | solution.py:34
  33.6 1.2 collective-permute-start.1
  34.8 2.3 collective-permute-done.22.refs_20_
  37.2 3.1 %collective-permute-done.20.refs_18_ = f32[1,512,128]{2,1,0:T(8,128)S(1)} collective-permute-done((f32[1,512,128]{2,1,0:T(8,128)S(1)}, f32[1,512,128]{2,1,0:T(8,128)S(1)}, u32[]{:S(2)}, u32[]{:S(2)}) %collective-permute-start.20) | collective-permute-done | bytes 262176 | tf_op jit(solution)/shard_map/ppermute | solution.py:34
  40.4 7.5 %collective-permute-start.11 = (f32[256,128]{1,0:T(8,128)S(1)}, f32[256,128]{1,0:T(8,128)S(1)}, u32[]{:S(2)}, u32[]{:S(2)}) collective-permute-start(f32[256,128]{1,0:T(8,128)S(1)} %get-tuple-element.51), channel_id=1, source_target_pairs={{0,96},{8,104},{16,112},{24,120},{32,0},{40,8},{48,16},{56,24},{64... | collective-permute-start | bytes 393224 | tf_op jit(solution)/shard_map/ppermute | solution.py:34
  47.8 5.8 %collective-permute-start.12 = (f32[256,128]{1,0:T(8,128)S(1)}, f32[256,128]{1,0:T(8,128)S(1)}, u32[]{:S(2)}, u32[]{:S(2)}) collective-permute-start(f32[256,128]{1,0:T(8,128)S(1)} %get-tuple-element.51), channel_id=1, source_target_pairs={{0,64},{8,72},{16,80},{24,88},{32,96},{40,104},{48,112},{56,120},{... | collective-permute-start | bytes 393224 | tf_op jit(solution)/shard_map/ppermute | solution.py:34
  53.7 1.6 collective-permute-start.23
  55.4 1.5 collective-permute-start.7
  56.9 1.2 collective-permute-done.12
  58.2 2.7 %collective-permute-start.6 = (f32[2,256,128]{2,1,0:T(8,128)S(1)}, f32[2,256,128]{2,1,0:T(8,128)S(1)}, u32[]{:S(2)}, u32[]{:S(2)}) collective-permute-start(f32[2,256,128]{2,1,0:T(8,128)S(1)} %pad_maximum_fusion.refs_0_), channel_id=1, source_target_pairs={{0,96},{8,104},{16,112},{24,120},{32,0},{40,8},{48,16},{56,24},{64... | collective-permute-start | bytes 786440 | tf_op jit(solution)/shard_map/ppermute | solution.py:34
  61.0 1.6 collective-permute-done.21.refs_19_
  63.5 1.3 collective-permute-start.14
  68.5 2.8 %collective-permute-done.4.refs_2_ = f32[2,256,128]{2,1,0:T(8,128)} collective-permute-done((f32[2,256,128]{2,1,0:T(8,128)S(1)}, f32[2,256,128]{2,1,0:T(8,128)}, u32[]{:S(2)}, u32[]{:S(2)}) %collective-permute-start.4) | collective-permute-done | bytes 262176 | tf_op jit(solution)/shard_map/ppermute | solution.py:34
  71.4 1.3 collective-permute-start.25
  73.7 1.1 collective-permute-start.8
  75.6 1.6 collective-permute-start.18
  78.5 1.9 collective-permute-done.8.refs_6_
  80.4 0.9 collective-permute-done.18.refs_15_
  81.4 3.0 %collective-permute-done.17.refs_14_ = f32[2,256,128]{2,1,0:T(8,128)} collective-permute-done((f32[2,256,128]{2,1,0:T(8,128)}, f32[2,256,128]{2,1,0:T(8,128)}, u32[]{:S(2)}, u32[]{:S(2)}) %collective-permute-start.17) | collective-permute-done | bytes 262176 | tf_op jit(solution)/shard_map/ppermute | solution.py:34
  84.4 0.9 copy-done.3
  85.3 0.9 copy-done.5
  86.3 0.9 copy-done.7
  87.2 0.9 copy-done.9
  88.2 0.9 copy-done.11
  89.1 11.5 %pair_weights.1 = (f32[4,64,1024]{2,1,0:T(8,128)S(1)}, f32[4,64,1024]{2,1,0:T(8,128)S(1)}) custom-call(s32[4,16]{1,0:T(4,128)S(1)} %pad_add_fusion.order.refs_0_, s32[8]{0:T(128)S(1)} %fusion.26.panel_order, s32[5]{0:T(128)S(1)} %pad_add_fusion.1.chips.where, f32[2,256,128]{2,1,0:T(8,128)S(1)} %pad_maximum_fusion.refs_0_, ...), custom_call_target="tpu_custom_call" | custom-call | flops 6442450944 | bytes 12582912 | tf_op jit(solution)/shard_map/pair_weights/pallas_call | solution.py:177
  100.7 5.9 %collective-permute-start.26 = (f32[4,64,1024]{2,1,0:T(8,128)S(1)}, f32[4,64,1024]{2,1,0:T(8,128)S(1)}, u32[]{:S(2)}, u32[]{:S(2)}) collective-permute-start(f32[4,64,1024]{2,1,0:T(8,128)S(1)} %get-tuple-element.18), channel_id=1, source_target_pairs={{0,1},{1,0},{2,3},{3,2},{4,5},{5,4},{6,7},{7,6},{8,9},{9,8},{10,11... | collective-permute-start | bytes 3145736 | tf_op jit(solution)/shard_map/ppermute | solution.py:38
  106.6 2.3 collective-permute-done.26
  109.1 1.9 collective-permute-start.28
  111.0 4.8 %collective-permute-start.30 = (f32[64,1024]{1,0:T(8,128)S(1)}, f32[64,1024]{1,0:T(8,128)S(1)}, u32[]{:S(2)}, u32[]{:S(2)}) collective-permute-start(f32[64,1024]{1,0:T(8,128)S(1)} %get-tuple-element.42), channel_id=1, source_target_pairs={{0,96},{1,120},{2,0},{3,24},{4,32},{5,56},{6,64},{7,88},{8,104},{9... | collective-permute-start | bytes 786440 | tf_op jit(solution)/shard_map/ppermute | solution.py:56
  115.8 3.1 %collective-permute-start.29 = (f32[64,1024]{1,0:T(8,128)S(1)}, f32[64,1024]{1,0:T(8,128)S(1)}, u32[]{:S(2)}, u32[]{:S(2)}) collective-permute-start(f32[64,1024]{1,0:T(8,128)S(1)} %get-tuple-element.43), channel_id=1, source_target_pairs={{0,64},{1,88},{2,96},{3,120},{4,0},{5,24},{6,32},{7,56},{8,72},{9,... | collective-permute-start | bytes 786440 | tf_op jit(solution)/shard_map/ppermute | solution.py:56
  118.9 3.7 %collective-permute-start.27 = (f32[64,1024]{1,0:T(8,128)S(1)}, f32[64,1024]{1,0:T(8,128)S(1)}, u32[]{:S(2)}, u32[]{:S(2)}) collective-permute-start(f32[64,1024]{1,0:T(8,128)S(1)} %get-tuple-element.44), channel_id=1, source_target_pairs={{0,0},{1,24},{2,32},{3,56},{4,64},{5,88},{6,96},{7,120},{8,8},{9,1... | collective-permute-start | bytes 786440 | tf_op jit(solution)/shard_map/ppermute | solution.py:56
  122.6 5.7 %collective-permute-done.29 = f32[64,1024]{1,0:T(8,128)S(1)} collective-permute-done((f32[64,1024]{1,0:T(8,128)S(1)}, f32[64,1024]{1,0:T(8,128)S(1)}, u32[]{:S(2)}, u32[]{:S(2)}) %collective-permute-start.29) | collective-permute-done | bytes 262176 | tf_op jit(solution)/shard_map/ppermute | solution.py:56
  128.4 2.1 collective-permute-start.32
  131.2 5.5 %collective-permute-start.41 = (f32[32,1024]{1,0:T(8,128)S(1)}, f32[32,1024]{1,0:T(8,128)S(1)}, u32[]{:S(2)}, u32[]{:S(2)}) collective-permute-start(f32[32,1024]{1,0:T(8,128)S(1)} %get-tuple-element.47), channel_id=1, source_target_pairs={{0,96},{8,104},{16,112},{24,120},{32,0},{40,8},{48,16},{56,24},{64... | collective-permute-start | bytes 393224 | tf_op jit(solution)/shard_map/ppermute | solution.py:34
  136.7 8.7 %collective-permute-start.42 = (f32[32,1024]{1,0:T(8,128)S(1)}, f32[32,1024]{1,0:T(8,128)S(1)}, u32[]{:S(2)}, u32[]{:S(2)}) collective-permute-start(f32[32,1024]{1,0:T(8,128)S(1)} %get-tuple-element.47), channel_id=1, source_target_pairs={{0,64},{8,72},{16,80},{24,88},{32,96},{40,104},{48,112},{56,120},{... | collective-permute-start | bytes 393224 | tf_op jit(solution)/shard_map/ppermute | solution.py:34
  145.5 1.4 collective-permute-start.35
  147.0 1.4 collective-permute-start.36
  149.0 3.2 %collective-permute-start.46 = (f32[2,32,1024]{2,1,0:T(8,128)S(1)}, f32[2,32,1024]{2,1,0:T(8,128)S(1)}, u32[]{:S(2)}, u32[]{:S(2)}) collective-permute-start(f32[2,32,1024]{2,1,0:T(8,128)S(1)} %pad_maximum_fusion.7.refs_10_), channel_id=1, source_target_pairs={{0,24},{8,0},{16,8},{24,16},{32,56},{40,32},{48,40},{56,48},{64,88... | collective-permute-start | bytes 786440 | tf_op jit(solution)/shard_map/ppermute | solution.py:34
  152.3 1.0 collective-permute-done.35.refs_4_
  153.3 1.2 collective-permute-start.43
  154.5 3.1 %collective-permute-done.36.refs_5_ = f32[2,32,1024]{2,1,0:T(8,128)S(1)} collective-permute-done((f32[2,32,1024]{2,1,0:T(8,128)S(1)}, f32[2,32,1024]{2,1,0:T(8,128)S(1)}, u32[]{:S(2)}, u32[]{:S(2)}) %collective-permute-start.36) | collective-permute-done | bytes 262176 | tf_op jit(solution)/shard_map/ppermute | solution.py:34
  157.6 3.7 %collective-permute-start.45 = (f32[2,32,1024]{2,1,0:T(8,128)S(1)}, f32[2,32,1024]{2,1,0:T(8,128)S(1)}, u32[]{:S(2)}, u32[]{:S(2)}) collective-permute-start(f32[2,32,1024]{2,1,0:T(8,128)S(1)} %pad_maximum_fusion.6.refs_9_), channel_id=1, source_target_pairs={{0,24},{8,0},{16,8},{24,16},{32,56},{40,32},{48,40},{56,48},{64,88... | collective-permute-start | bytes 786440 | tf_op jit(solution)/shard_map/ppermute | solution.py:34
  161.4 1.5 collective-permute-start.39
  162.9 2.2 collective-permute-start.48
  165.2 1.8 collective-permute-done.39.refs_8_
  166.9 2.7 %collective-permute-done.38.refs_7_ = f32[2,32,1024]{2,1,0:T(8,128)S(1)} collective-permute-done((f32[2,32,1024]{2,1,0:T(8,128)S(1)}, f32[2,32,1024]{2,1,0:T(8,128)S(1)}, u32[]{:S(2)}, u32[]{:S(2)}) %collective-permute-start.38) | collective-permute-done | bytes 262176 | tf_op jit(solution)/shard_map/ppermute | solution.py:34
  169.6 1.6 collective-permute-done.48.refs_16_
  172.1 14.1 %term.2 = (f32[2,1024,128]{2,1,0:T(8,128)}, f32[2,1024,128]{2,1,0:T(8,128)}, f32[2,1024,128]{2,1,0:T(8,128)}, f32[2,1024,128]{2,1,0:T(8,128)}, bf16[1024,1024]{1,0:T(8,128)(2,1)}, /*index=5*/bf16[1024,1024]{1,0:T(8,128)(2,1)}) custom-call(s32[5]{0:T(128)} %copy-done.12, s32[4,16]{1,0:T(4,128)} %copy-done.1, f32[2,32,1024]{2,1,0:T(8,128)} %copy-done.19, ...), custom_call_target="tpu_custom_call" | custom-call | flops 6442450944 | bytes 16777216 | tf_op jit(solution)/shard_map/term/pallas_call | solution.py:287
  186.2 4.4 %collective-permute-start.49 = (f32[2,1024,128]{2,1,0:T(8,128)}, f32[2,1024,128]{2,1,0:T(8,128)S(1)}, u32[]{:S(2)}, u32[]{:S(2)}) collective-permute-start(f32[2,1024,128]{2,1,0:T(8,128)} %get-tuple-element.22), channel_id=1, source_target_pairs={{0,1},{1,0},{2,3},{3,2},{4,5},{5,4},{6,7},{7,6},{8,9},{9,8},{10,11... | collective-permute-start | bytes 3145736 | tf_op jit(solution)/shard_map/ppermute | solution.py:38
  190.6 2.4 collective-permute-done.49
  193.0 2.3 fusion.13
  195.3 11.7 %term.3 = (f32[2,1024,128]{2,1,0:T(8,128)}, f32[2,1024,128]{2,1,0:T(8,128)}, f32[2,1024,128]{2,1,0:T(8,128)}, f32[2,1024,128]{2,1,0:T(8,128)}) custom-call(s32[5]{0:T(128)} %copy-done.12, f32[2048,1024]{1,0:T(8,128)} %refs_0_.1, bf16[1024,1024]{1,0:T(8,128)(2,1)} %get-tuple-element.19.refs_1_.refs_3_, bf16[1024,1024]{1,0:T(8,128)(2,1)} %get-tuple-element.20.refs_2_.refs_4_, ...), custom_call_target="tpu_custom_call" | custom-call | flops 6442450944 | bytes 16777216 | tf_op jit(solution)/shard_map/term/pallas_call | solution.py:287
  208.1 2.2 collective-permute-start.57
  211.1 11.2 %collective-permute-done.53 = f32[1024,128]{1,0:T(8,128)S(1)} collective-permute-done((f32[1024,128]{1,0:T(8,128)S(1)}, f32[1024,128]{1,0:T(8,128)S(1)}, u32[]{:S(2)}, u32[]{:S(2)}) %collective-permute-start.53) | collective-permute-done | bytes 524320 | tf_op jit(solution)/shard_map/ppermute | solution.py:34
  222.4 1.5 collective-permute-start.54
  224.0 1.2 collective-permute-start.58
  225.2 8.3 %collective-permute-done.56 = f32[1024,128]{1,0:T(8,128)S(1)} collective-permute-done((f32[1024,128]{1,0:T(8,128)S(1)}, f32[1024,128]{1,0:T(8,128)S(1)}, u32[]{:S(2)}, u32[]{:S(2)}) %collective-permute-start.56) | collective-permute-done | bytes 524320 | tf_op jit(solution)/shard_map/ppermute | solution.py:34
  234.2 10.6 %collective-permute-done.54 = f32[1024,128]{1,0:T(8,128)S(1)} collective-permute-done((f32[1024,128]{1,0:T(8,128)S(1)}, f32[1024,128]{1,0:T(8,128)S(1)}, u32[]{:S(2)}, u32[]{:S(2)}) %collective-permute-start.54) | collective-permute-done | bytes 524320 | tf_op jit(solution)/shard_map/ppermute | solution.py:34
  245.6 1.0 maximum_negate_fusion
  (185 shorter events, 17.7 us)
Async XLA Ops:
  5.8 18.0 %all-to-all-start = ((f32[16,64,128]{2,1,0:T(8,128)}), f32[16,64,128]{2,1,0:T(8,128)S(1)}, u32[]{:S(2)}, u32[]{:S(2)}) async-start(f32[16,64,128]{2,1,0:T(8,128)} %bitcast.2), calls=%async_computation | async-start | bytes 1048576 | tf_op jit(solution)/shard_map/all_to_all | solution.py:319
  23.8 44.7 %copy-start.35 = (s32[4]{0:T(128)S(1)}, s32[4]{0:T(128)}, u32[]{:S(2)}) copy-start(s32[4]{0:T(128)} %constant.139.clone) | copy-start | bytes 52
  24.9 8.4 %collective-permute-start = (f32[512,128]{1,0:T(8,128)S(1)}, f32[512,128]{1,0:T(8,128)S(1)}, u32[]{:S(2)}, u32[]{:S(2)}) collective-permute-start(f32[512,128]{1,0:T(8,128)S(1)} %gather_fusion.1), channel_id=1, source_target_pairs={{0,0},{1,24},{2,32},{3,56},{4,64},{5,88},{6,96},{7,120},{8,8},{9,1... | collective-permute-start | bytes 786440 | tf_op jit(solution)/shard_map/ppermute | solution.py:56
  29.1 8.1 %collective-permute-start.22 = (f32[1,512,128]{2,1,0:T(8,128)S(1)}, f32[1,512,128]{2,1,0:T(8,128)S(1)}, u32[]{:S(2)}, u32[]{:S(2)}) collective-permute-start(f32[1,512,128]{2,1,0:T(8,128)S(1)} %bitcast.65), channel_id=1, source_target_pairs={{0,6},{1,7},{2,0},{3,1},{4,2},{5,3},{6,4},{7,5},{8,14},{9,15},{10,... | collective-permute-start | bytes 786440 | tf_op jit(solution)/shard_map/ppermute | solution.py:34
  32.1 8.2 %collective-permute-start.20 = (f32[1,512,128]{2,1,0:T(8,128)S(1)}, f32[1,512,128]{2,1,0:T(8,128)S(1)}, u32[]{:S(2)}, u32[]{:S(2)}) collective-permute-start(f32[1,512,128]{2,1,0:T(8,128)S(1)} %bitcast.66), channel_id=1, source_target_pairs={{0,2},{1,3},{2,4},{3,5},{4,6},{5,7},{6,0},{7,1},{8,10},{9,11},{10,... | collective-permute-start | bytes 786440 | tf_op jit(solution)/shard_map/ppermute | solution.py:34
  32.4 21.4 %collective-permute-start.19 = (f32[1,512,128]{2,1,0:T(8,128)S(1)}, f32[1,512,128]{2,1,0:T(8,128)S(1)}, u32[]{:S(2)}, u32[]{:S(2)}) collective-permute-start(f32[1,512,128]{2,1,0:T(8,128)S(1)} %bitcast.67), channel_id=1, source_target_pairs={{0,1},{1,0},{2,3},{3,2},{4,5},{5,4},{6,7},{7,6},{8,9},{9,8},{10,11... | collective-permute-start | bytes 786440 | tf_op jit(solution)/shard_map/ppermute | solution.py:38
  33.3 7.0 %collective-permute-start.2 = (f32[256,128]{1,0:T(8,128)S(1)}, f32[256,128]{1,0:T(8,128)S(1)}, u32[]{:S(2)}, u32[]{:S(2)}) collective-permute-start(f32[256,128]{1,0:T(8,128)S(1)} %get-tuple-element.52), channel_id=1, source_target_pairs={{0,24},{8,0},{16,8},{24,16},{32,56},{40,32},{48,40},{56,48},{64,88... | collective-permute-start | bytes 393224 | tf_op jit(solution)/shard_map/ppermute | solution.py:34
  33.6 14.2 %collective-permute-start.1 = (f32[256,128]{1,0:T(8,128)S(1)}, f32[256,128]{1,0:T(8,128)S(1)}, u32[]{:S(2)}, u32[]{:S(2)}) collective-permute-start(f32[256,128]{1,0:T(8,128)S(1)} %get-tuple-element.52), channel_id=1, source_target_pairs={{0,8},{8,16},{16,24},{24,0},{32,40},{40,48},{48,56},{56,32},{64,72... | collective-permute-start | bytes 393224 | tf_op jit(solution)/shard_map/ppermute | solution.py:34
  37.2 10.7 %collective-permute-start.3 = (f32[256,128]{1,0:T(8,128)S(1)}, f32[256,128]{1,0:T(8,128)S(1)}, u32[]{:S(2)}, u32[]{:S(2)}) collective-permute-start(f32[256,128]{1,0:T(8,128)S(1)} %get-tuple-element.52), channel_id=1, source_target_pairs={{0,16},{8,24},{16,0},{24,8},{32,48},{40,56},{48,32},{56,40},{64,80... | collective-permute-start | bytes 393224 | tf_op jit(solution)/shard_map/ppermute | solution.py:34
  40.3 17.9 %collective-permute-start.24 = (f32[1,512,128]{2,1,0:T(8,128)S(1)}, f32[1,512,128]{2,1,0:T(8,128)S(1)}, u32[]{:S(2)}, u32[]{:S(2)}) collective-permute-start(f32[1,512,128]{2,1,0:T(8,128)S(1)} %collective-permute-done.20.refs_18_), channel_id=1, source_target_pairs={{0,2},{1,3},{2,4},{3,5},{4,6},{5,7},{6,0},{7,1},{8,10},{9,11},{10,... | collective-permute-start | bytes 786440 | tf_op jit(solution)/shard_map/ppermute | solution.py:34
  40.4 15.0 %collective-permute-start.11 = (f32[256,128]{1,0:T(8,128)S(1)}, f32[256,128]{1,0:T(8,128)S(1)}, u32[]{:S(2)}, u32[]{:S(2)}) collective-permute-start(f32[256,128]{1,0:T(8,128)S(1)} %get-tuple-element.51), channel_id=1, source_target_pairs={{0,96},{8,104},{16,112},{24,120},{32,0},{40,8},{48,16},{56,24},{64... | collective-permute-start | bytes 393224 | tf_op jit(solution)/shard_map/ppermute | solution.py:34
  47.8 7.5 %collective-permute-start.10 = (f32[256,128]{1,0:T(8,128)S(1)}, f32[256,128]{1,0:T(8,128)S(1)}, u32[]{:S(2)}, u32[]{:S(2)}) collective-permute-start(f32[256,128]{1,0:T(8,128)S(1)} %get-tuple-element.51), channel_id=1, source_target_pairs={{0,32},{8,40},{16,48},{24,56},{32,64},{40,72},{48,80},{56,88},{64,... | collective-permute-start | bytes 393224 | tf_op jit(solution)/shard_map/ppermute | solution.py:34
  47.8 10.3 %collective-permute-start.12 = (f32[256,128]{1,0:T(8,128)S(1)}, f32[256,128]{1,0:T(8,128)S(1)}, u32[]{:S(2)}, u32[]{:S(2)}) collective-permute-start(f32[256,128]{1,0:T(8,128)S(1)} %get-tuple-element.51), channel_id=1, source_target_pairs={{0,64},{8,72},{16,80},{24,88},{32,96},{40,104},{48,112},{56,120},{... | collective-permute-start | bytes 393224 | tf_op jit(solution)/shard_map/ppermute | solution.py:34
  53.7 7.2 %collective-permute-start.23 = (f32[1,512,128]{2,1,0:T(8,128)S(1)}, f32[1,512,128]{2,1,0:T(8,128)}, u32[]{:S(2)}, u32[]{:S(2)}) collective-permute-start(f32[1,512,128]{2,1,0:T(8,128)S(1)} %collective-permute-done.19.refs_17_), channel_id=1, source_target_pairs={{0,6},{1,7},{2,0},{3,1},{4,2},{5,3},{6,4},{7,5},{8,14},{9,15},{10,... | collective-permute-start | bytes 786440 | tf_op jit(solution)/shard_map/ppermute | solution.py:34
  55.4 7.3 %collective-permute-start.21 = (f32[1,512,128]{2,1,0:T(8,128)S(1)}, f32[1,512,128]{2,1,0:T(8,128)S(1)}, u32[]{:S(2)}, u32[]{:S(2)}) collective-permute-start(f32[1,512,128]{2,1,0:T(8,128)S(1)} %collective-permute-done.19.refs_17_), channel_id=1, source_target_pairs={{0,2},{1,3},{2,4},{3,5},{4,6},{5,7},{6,0},{7,1},{8,10},{9,11},{10,... | collective-permute-start | bytes 786440 | tf_op jit(solution)/shard_map/ppermute | solution.py:34
  55.4 8.1 %collective-permute-start.7 = (f32[2,256,128]{2,1,0:T(8,128)S(1)}, f32[2,256,128]{2,1,0:T(8,128)}, u32[]{:S(2)}, u32[]{:S(2)}) collective-permute-start(f32[2,256,128]{2,1,0:T(8,128)S(1)} %pad_maximum_fusion.1.refs_1_), channel_id=1, source_target_pairs={{0,96},{8,104},{16,112},{24,120},{32,0},{40,8},{48,16},{56,24},{64... | collective-permute-start | bytes 786440 | tf_op jit(solution)/shard_map/ppermute | solution.py:34
  58.2 7.5 %collective-permute-start.5 = (f32[2,256,128]{2,1,0:T(8,128)S(1)}, f32[2,256,128]{2,1,0:T(8,128)S(1)}, u32[]{:S(2)}, u32[]{:S(2)}) collective-permute-start(f32[2,256,128]{2,1,0:T(8,128)S(1)} %pad_maximum_fusion.1.refs_1_), channel_id=1, source_target_pairs={{0,32},{8,40},{16,48},{24,56},{32,64},{40,72},{48,80},{56,88},{64,... | collective-permute-start | bytes 786440 | tf_op jit(solution)/shard_map/ppermute | solution.py:34
  58.2 8.8 %collective-permute-start.6 = (f32[2,256,128]{2,1,0:T(8,128)S(1)}, f32[2,256,128]{2,1,0:T(8,128)S(1)}, u32[]{:S(2)}, u32[]{:S(2)}) collective-permute-start(f32[2,256,128]{2,1,0:T(8,128)S(1)} %pad_maximum_fusion.refs_0_), channel_id=1, source_target_pairs={{0,96},{8,104},{16,112},{24,120},{32,0},{40,8},{48,16},{56,24},{64... | collective-permute-start | bytes 786440 | tf_op jit(solution)/shard_map/ppermute | solution.py:34
  60.9 39.8 %copy-start.1 = (s32[4,16]{1,0:T(4,128)}, s32[4,16]{1,0:T(4,128)S(1)}, u32[]{:S(2)}) copy-start(s32[4,16]{1,0:T(4,128)S(1)} %pad_add_fusion.order.refs_0_) | copy-start | bytes 772
  60.9 10.4 %collective-permute-start.4 = (f32[2,256,128]{2,1,0:T(8,128)S(1)}, f32[2,256,128]{2,1,0:T(8,128)}, u32[]{:S(2)}, u32[]{:S(2)}) collective-permute-start(f32[2,256,128]{2,1,0:T(8,128)S(1)} %pad_maximum_fusion.refs_0_), channel_id=1, source_target_pairs={{0,32},{8,40},{16,48},{24,56},{32,64},{40,72},{48,80},{56,88},{64,... | collective-permute-start | bytes 786440 | tf_op jit(solution)/shard_map/ppermute | solution.py:34
  63.3 9.3 %collective-permute-start.16 = (f32[2,256,128]{2,1,0:T(8,128)S(1)}, f32[2,256,128]{2,1,0:T(8,128)}, u32[]{:S(2)}, u32[]{:S(2)}) collective-permute-start(f32[2,256,128]{2,1,0:T(8,128)S(1)} %pad_maximum_fusion.3.refs_9_), channel_id=1, source_target_pairs={{0,24},{8,0},{16,8},{24,16},{32,56},{40,32},{48,40},{56,48},{64,88... | collective-permute-start | bytes 786440 | tf_op jit(solution)/shard_map/ppermute | solution.py:34
  63.5 9.5 %collective-permute-start.14 = (f32[2,256,128]{2,1,0:T(8,128)S(1)}, f32[2,256,128]{2,1,0:T(8,128)S(1)}, u32[]{:S(2)}, u32[]{:S(2)}) collective-permute-start(f32[2,256,128]{2,1,0:T(8,128)S(1)} %pad_maximum_fusion.3.refs_9_), channel_id=1, source_target_pairs={{0,8},{8,16},{16,24},{24,0},{32,40},{40,48},{48,56},{56,32},{64,72... | collective-permute-start | bytes 786440 | tf_op jit(solution)/shard_map/ppermute | solution.py:34
  66.3 8.5 %collective-permute-start.15 = (f32[2,256,128]{2,1,0:T(8,128)S(1)}, f32[2,256,128]{2,1,0:T(8,128)S(1)}, u32[]{:S(2)}, u32[]{:S(2)}) collective-permute-start(f32[2,256,128]{2,1,0:T(8,128)S(1)} %pad_maximum_fusion.2.refs_8_), channel_id=1, source_target_pairs={{0,24},{8,0},{16,8},{24,16},{32,56},{40,32},{48,40},{56,48},{64,88... | collective-permute-start | bytes 786440 | tf_op jit(solution)/shard_map/ppermute | solution.py:34
  67.7 9.6 %collective-permute-start.13 = (f32[2,256,128]{2,1,0:T(8,128)S(1)}, f32[2,256,128]{2,1,0:T(8,128)}, u32[]{:S(2)}, u32[]{:S(2)}) collective-permute-start(f32[2,256,128]{2,1,0:T(8,128)S(1)} %pad_maximum_fusion.2.refs_8_), channel_id=1, source_target_pairs={{0,8},{8,16},{16,24},{24,0},{32,40},{40,48},{48,56},{56,32},{64,72... | collective-permute-start | bytes 786440 | tf_op jit(solution)/shard_map/ppermute | solution.py:34
  71.4 6.3 %collective-permute-start.25 = (f32[1,512,128]{2,1,0:T(8,128)}, f32[1,512,128]{2,1,0:T(8,128)}, u32[]{:S(2)}, u32[]{:S(2)}) collective-permute-start(f32[1,512,128]{2,1,0:T(8,128)} %collective-permute-done.23.refs_21_), channel_id=1, source_target_pairs={{0,6},{1,7},{2,0},{3,1},{4,2},{5,3},{6,4},{7,5},{8,14},{9,15},{10,... | collective-permute-start | bytes 786440 | tf_op jit(solution)/shard_map/ppermute | solution.py:34
  72.7 5.8 %collective-permute-start.9 = (f32[2,256,128]{2,1,0:T(8,128)}, f32[2,256,128]{2,1,0:T(8,128)}, u32[]{:S(2)}, u32[]{:S(2)}) collective-permute-start(f32[2,256,128]{2,1,0:T(8,128)} %collective-permute-done.7.refs_5_), channel_id=1, source_target_pairs={{0,96},{8,104},{16,112},{24,120},{32,0},{40,8},{48,16},{56,24},{64... | collective-permute-start | bytes 786440 | tf_op jit(solution)/shard_map/ppermute | solution.py:34
  73.7 6.7 %collective-permute-start.8 = (f32[2,256,128]{2,1,0:T(8,128)}, f32[2,256,128]{2,1,0:T(8,128)}, u32[]{:S(2)}, u32[]{:S(2)}) collective-permute-start(f32[2,256,128]{2,1,0:T(8,128)} %collective-permute-done.4.refs_2_), channel_id=1, source_target_pairs={{0,32},{8,40},{16,48},{24,56},{32,64},{40,72},{48,80},{56,88},{64,... | collective-permute-start | bytes 786440 | tf_op jit(solution)/shard_map/ppermute | solution.py:34
  75.6 5.8 %collective-permute-start.18 = (f32[2,256,128]{2,1,0:T(8,128)}, f32[2,256,128]{2,1,0:T(8,128)}, u32[]{:S(2)}, u32[]{:S(2)}) collective-permute-start(f32[2,256,128]{2,1,0:T(8,128)} %collective-permute-done.16.refs_13_), channel_id=1, source_target_pairs={{0,24},{8,0},{16,8},{24,16},{32,56},{40,32},{48,40},{56,48},{64,88... | collective-permute-start | bytes 786440 | tf_op jit(solution)/shard_map/ppermute | solution.py:34
  77.3 7.0 %collective-permute-start.17 = (f32[2,256,128]{2,1,0:T(8,128)}, f32[2,256,128]{2,1,0:T(8,128)}, u32[]{:S(2)}, u32[]{:S(2)}) collective-permute-start(f32[2,256,128]{2,1,0:T(8,128)} %collective-permute-done.13.refs_10_), channel_id=1, source_target_pairs={{0,8},{8,16},{16,24},{24,0},{32,40},{40,48},{48,56},{56,32},{64,72... | collective-permute-start | bytes 786440 | tf_op jit(solution)/shard_map/ppermute | solution.py:34
  100.7 8.2 %collective-permute-start.26 = (f32[4,64,1024]{2,1,0:T(8,128)S(1)}, f32[4,64,1024]{2,1,0:T(8,128)S(1)}, u32[]{:S(2)}, u32[]{:S(2)}) collective-permute-start(f32[4,64,1024]{2,1,0:T(8,128)S(1)} %get-tuple-element.18), channel_id=1, source_target_pairs={{0,1},{1,0},{2,3},{3,2},{4,5},{5,4},{6,7},{7,6},{8,9},{9,8},{10,11... | collective-permute-start | bytes 3145736 | tf_op jit(solution)/shard_map/ppermute | solution.py:38
  109.1 13.5 %collective-permute-start.28 = (f32[64,1024]{1,0:T(8,128)S(1)}, f32[64,1024]{1,0:T(8,128)S(1)}, u32[]{:S(2)}, u32[]{:S(2)}) collective-permute-start(f32[64,1024]{1,0:T(8,128)S(1)} %get-tuple-element.41), channel_id=1, source_target_pairs={{0,32},{1,56},{2,64},{3,88},{4,96},{5,120},{6,0},{7,24},{8,40},{9,... | collective-permute-start | bytes 786440 | tf_op jit(solution)/shard_map/ppermute | solution.py:56
  111.0 11.6 %collective-permute-start.30 = (f32[64,1024]{1,0:T(8,128)S(1)}, f32[64,1024]{1,0:T(8,128)S(1)}, u32[]{:S(2)}, u32[]{:S(2)}) collective-permute-start(f32[64,1024]{1,0:T(8,128)S(1)} %get-tuple-element.42), channel_id=1, source_target_pairs={{0,96},{1,120},{2,0},{3,24},{4,32},{5,56},{6,64},{7,88},{8,104},{9... | collective-permute-start | bytes 786440 | tf_op jit(solution)/shard_map/ppermute | solution.py:56
  115.8 12.5 %collective-permute-start.29 = (f32[64,1024]{1,0:T(8,128)S(1)}, f32[64,1024]{1,0:T(8,128)S(1)}, u32[]{:S(2)}, u32[]{:S(2)}) collective-permute-start(f32[64,1024]{1,0:T(8,128)S(1)} %get-tuple-element.43), channel_id=1, source_target_pairs={{0,64},{1,88},{2,96},{3,120},{4,0},{5,24},{6,32},{7,56},{8,72},{9,... | collective-permute-start | bytes 786440 | tf_op jit(solution)/shard_map/ppermute | solution.py:56
  118.9 9.4 %collective-permute-start.27 = (f32[64,1024]{1,0:T(8,128)S(1)}, f32[64,1024]{1,0:T(8,128)S(1)}, u32[]{:S(2)}, u32[]{:S(2)}) collective-permute-start(f32[64,1024]{1,0:T(8,128)S(1)} %get-tuple-element.44), channel_id=1, source_target_pairs={{0,0},{1,24},{2,32},{3,56},{4,64},{5,88},{6,96},{7,120},{8,8},{9,1... | collective-permute-start | bytes 786440 | tf_op jit(solution)/shard_map/ppermute | solution.py:56
  128.4 8.3 %collective-permute-start.32 = (f32[32,1024]{1,0:T(8,128)S(1)}, f32[32,1024]{1,0:T(8,128)S(1)}, u32[]{:S(2)}, u32[]{:S(2)}) collective-permute-start(f32[32,1024]{1,0:T(8,128)S(1)} %get-tuple-element.48), channel_id=1, source_target_pairs={{0,24},{8,0},{16,8},{24,16},{32,56},{40,32},{48,40},{56,48},{64,88... | collective-permute-start | bytes 393224 | tf_op jit(solution)/shard_map/ppermute | solution.py:34
  130.5 14.9 %collective-permute-start.33 = (f32[32,1024]{1,0:T(8,128)S(1)}, f32[32,1024]{1,0:T(8,128)S(1)}, u32[]{:S(2)}, u32[]{:S(2)}) collective-permute-start(f32[32,1024]{1,0:T(8,128)S(1)} %get-tuple-element.48), channel_id=1, source_target_pairs={{0,16},{8,24},{16,0},{24,8},{32,48},{40,56},{48,32},{56,40},{64,80... | collective-permute-start | bytes 393224 | tf_op jit(solution)/shard_map/ppermute | solution.py:34
  130.5 15.0 %collective-permute-start.31 = (f32[32,1024]{1,0:T(8,128)S(1)}, f32[32,1024]{1,0:T(8,128)S(1)}, u32[]{:S(2)}, u32[]{:S(2)}) collective-permute-start(f32[32,1024]{1,0:T(8,128)S(1)} %get-tuple-element.48), channel_id=1, source_target_pairs={{0,8},{8,16},{16,24},{24,0},{32,40},{40,48},{48,56},{56,32},{64,72... | collective-permute-start | bytes 393224 | tf_op jit(solution)/shard_map/ppermute | solution.py:34
  131.2 15.8 %collective-permute-start.41 = (f32[32,1024]{1,0:T(8,128)S(1)}, f32[32,1024]{1,0:T(8,128)S(1)}, u32[]{:S(2)}, u32[]{:S(2)}) collective-permute-start(f32[32,1024]{1,0:T(8,128)S(1)} %get-tuple-element.47), channel_id=1, source_target_pairs={{0,96},{8,104},{16,112},{24,120},{32,0},{40,8},{48,16},{56,24},{64... | collective-permute-start | bytes 393224 | tf_op jit(solution)/shard_map/ppermute | solution.py:34
  136.7 12.2 %collective-permute-start.40 = (f32[32,1024]{1,0:T(8,128)S(1)}, f32[32,1024]{1,0:T(8,128)S(1)}, u32[]{:S(2)}, u32[]{:S(2)}) collective-permute-start(f32[32,1024]{1,0:T(8,128)S(1)} %get-tuple-element.47), channel_id=1, source_target_pairs={{0,32},{8,40},{16,48},{24,56},{32,64},{40,72},{48,80},{56,88},{64,... | collective-permute-start | bytes 393224 | tf_op jit(solution)/shard_map/ppermute | solution.py:34
  136.7 11.7 %collective-permute-start.42 = (f32[32,1024]{1,0:T(8,128)S(1)}, f32[32,1024]{1,0:T(8,128)S(1)}, u32[]{:S(2)}, u32[]{:S(2)}) collective-permute-start(f32[32,1024]{1,0:T(8,128)S(1)} %get-tuple-element.47), channel_id=1, source_target_pairs={{0,64},{8,72},{16,80},{24,88},{32,96},{40,104},{48,112},{56,120},{... | collective-permute-start | bytes 393224 | tf_op jit(solution)/shard_map/ppermute | solution.py:34
  145.4 26.6 %copy-start.18 = (f32[2,32,1024]{2,1,0:T(8,128)}, f32[2,32,1024]{2,1,0:T(8,128)S(1)}, u32[]{:S(2)}) copy-start(f32[2,32,1024]{2,1,0:T(8,128)S(1)} %pad_maximum_fusion.5.refs_2_) | copy-start | bytes 786436
  145.4 6.8 %collective-permute-start.37 = (f32[2,32,1024]{2,1,0:T(8,128)S(1)}, f32[2,32,1024]{2,1,0:T(8,128)S(1)}, u32[]{:S(2)}, u32[]{:S(2)}) collective-permute-start(f32[2,32,1024]{2,1,0:T(8,128)S(1)} %pad_maximum_fusion.5.refs_2_), channel_id=1, source_target_pairs={{0,96},{8,104},{16,112},{24,120},{32,0},{40,8},{48,16},{56,24},{64... | collective-permute-start | bytes 786440 | tf_op jit(solution)/shard_map/ppermute | solution.py:34
  145.5 7.8 %collective-permute-start.35 = (f32[2,32,1024]{2,1,0:T(8,128)S(1)}, f32[2,32,1024]{2,1,0:T(8,128)S(1)}, u32[]{:S(2)}, u32[]{:S(2)}) collective-permute-start(f32[2,32,1024]{2,1,0:T(8,128)S(1)} %pad_maximum_fusion.5.refs_2_), channel_id=1, source_target_pairs={{0,32},{8,40},{16,48},{24,56},{32,64},{40,72},{48,80},{56,88},{64,... | collective-permute-start | bytes 786440 | tf_op jit(solution)/shard_map/ppermute | solution.py:34
  147.0 25.0 %copy-start.19 = (f32[2,32,1024]{2,1,0:T(8,128)}, f32[2,32,1024]{2,1,0:T(8,128)S(1)}, u32[]{:S(2)}) copy-start(f32[2,32,1024]{2,1,0:T(8,128)S(1)} %pad_maximum_fusion.4.refs_1_) | copy-start | bytes 786436
  147.0 10.6 %collective-permute-start.36 = (f32[2,32,1024]{2,1,0:T(8,128)S(1)}, f32[2,32,1024]{2,1,0:T(8,128)S(1)}, u32[]{:S(2)}, u32[]{:S(2)}) collective-permute-start(f32[2,32,1024]{2,1,0:T(8,128)S(1)} %pad_maximum_fusion.4.refs_1_), channel_id=1, source_target_pairs={{0,96},{8,104},{16,112},{24,120},{32,0},{40,8},{48,16},{56,24},{64... | collective-permute-start | bytes 786440 | tf_op jit(solution)/shard_map/ppermute | solution.py:34
  148.4 13.0 %collective-permute-start.34 = (f32[2,32,1024]{2,1,0:T(8,128)S(1)}, f32[2,32,1024]{2,1,0:T(8,128)S(1)}, u32[]{:S(2)}, u32[]{:S(2)}) collective-permute-start(f32[2,32,1024]{2,1,0:T(8,128)S(1)} %pad_maximum_fusion.4.refs_1_), channel_id=1, source_target_pairs={{0,32},{8,40},{16,48},{24,56},{32,64},{40,72},{48,80},{56,88},{64,... | collective-permute-start | bytes 786440 | tf_op jit(solution)/shard_map/ppermute | solution.py:34
  149.0 13.9 %collective-permute-start.46 = (f32[2,32,1024]{2,1,0:T(8,128)S(1)}, f32[2,32,1024]{2,1,0:T(8,128)S(1)}, u32[]{:S(2)}, u32[]{:S(2)}) collective-permute-start(f32[2,32,1024]{2,1,0:T(8,128)S(1)} %pad_maximum_fusion.7.refs_10_), channel_id=1, source_target_pairs={{0,24},{8,0},{16,8},{24,16},{32,56},{40,32},{48,40},{56,48},{64,88... | collective-permute-start | bytes 786440 | tf_op jit(solution)/shard_map/ppermute | solution.py:34
  152.2 10.6 %collective-permute-start.44 = (f32[2,32,1024]{2,1,0:T(8,128)S(1)}, f32[2,32,1024]{2,1,0:T(8,128)S(1)}, u32[]{:S(2)}, u32[]{:S(2)}) collective-permute-start(f32[2,32,1024]{2,1,0:T(8,128)S(1)} %pad_maximum_fusion.7.refs_10_), channel_id=1, source_target_pairs={{0,8},{8,16},{16,24},{24,0},{32,40},{40,48},{48,56},{56,32},{64,72... | collective-permute-start | bytes 786440 | tf_op jit(solution)/shard_map/ppermute | solution.py:34
  153.3 11.8 %collective-permute-start.43 = (f32[2,32,1024]{2,1,0:T(8,128)S(1)}, f32[2,32,1024]{2,1,0:T(8,128)S(1)}, u32[]{:S(2)}, u32[]{:S(2)}) collective-permute-start(f32[2,32,1024]{2,1,0:T(8,128)S(1)} %pad_maximum_fusion.6.refs_9_), channel_id=1, source_target_pairs={{0,8},{8,16},{16,24},{24,0},{32,40},{40,48},{48,56},{56,32},{64,72... | collective-permute-start | bytes 786440 | tf_op jit(solution)/shard_map/ppermute | solution.py:34
  157.6 7.5 %collective-permute-start.45 = (f32[2,32,1024]{2,1,0:T(8,128)S(1)}, f32[2,32,1024]{2,1,0:T(8,128)S(1)}, u32[]{:S(2)}, u32[]{:S(2)}) collective-permute-start(f32[2,32,1024]{2,1,0:T(8,128)S(1)} %pad_maximum_fusion.6.refs_9_), channel_id=1, source_target_pairs={{0,24},{8,0},{16,8},{24,16},{32,56},{40,32},{48,40},{56,48},{64,88... | collective-permute-start | bytes 786440 | tf_op jit(solution)/shard_map/ppermute | solution.py:34
  161.4 5.6 %collective-permute-start.39 = (f32[2,32,1024]{2,1,0:T(8,128)S(1)}, f32[2,32,1024]{2,1,0:T(8,128)S(1)}, u32[]{:S(2)}, u32[]{:S(2)}) collective-permute-start(f32[2,32,1024]{2,1,0:T(8,128)S(1)} %collective-permute-done.37.refs_6_), channel_id=1, source_target_pairs={{0,96},{8,104},{16,112},{24,120},{32,0},{40,8},{48,16},{56,24},{64... | collective-permute-start | bytes 786440 | tf_op jit(solution)/shard_map/ppermute | solution.py:34
  162.9 6.8 %collective-permute-start.38 = (f32[2,32,1024]{2,1,0:T(8,128)S(1)}, f32[2,32,1024]{2,1,0:T(8,128)S(1)}, u32[]{:S(2)}, u32[]{:S(2)}) collective-permute-start(f32[2,32,1024]{2,1,0:T(8,128)S(1)} %collective-permute-done.34.refs_3_), channel_id=1, source_target_pairs={{0,32},{8,40},{16,48},{24,56},{32,64},{40,72},{48,80},{56,88},{64,... | collective-permute-start | bytes 786440 | tf_op jit(solution)/shard_map/ppermute | solution.py:34
  162.9 8.4 %collective-permute-start.48 = (f32[2,32,1024]{2,1,0:T(8,128)S(1)}, f32[2,32,1024]{2,1,0:T(8,128)S(1)}, u32[]{:S(2)}, u32[]{:S(2)}) collective-permute-start(f32[2,32,1024]{2,1,0:T(8,128)S(1)} %collective-permute-done.46.refs_14_), channel_id=1, source_target_pairs={{0,24},{8,0},{16,8},{24,16},{32,56},{40,32},{48,40},{56,48},{64,88... | collective-permute-start | bytes 786440 | tf_op jit(solution)/shard_map/ppermute | solution.py:34
  165.1 6.9 %collective-permute-start.47 = (f32[2,32,1024]{2,1,0:T(8,128)S(1)}, f32[2,32,1024]{2,1,0:T(8,128)}, u32[]{:S(2)}, u32[]{:S(2)}) collective-permute-start(f32[2,32,1024]{2,1,0:T(8,128)S(1)} %collective-permute-done.43.refs_11_), channel_id=1, source_target_pairs={{0,8},{8,16},{16,24},{24,0},{32,40},{40,48},{48,56},{56,32},{64,72... | collective-permute-start | bytes 786440 | tf_op jit(solution)/shard_map/ppermute | solution.py:34
  186.2 6.9 %collective-permute-start.49 = (f32[2,1024,128]{2,1,0:T(8,128)}, f32[2,1024,128]{2,1,0:T(8,128)S(1)}, u32[]{:S(2)}, u32[]{:S(2)}) collective-permute-start(f32[2,1024,128]{2,1,0:T(8,128)} %get-tuple-element.22), channel_id=1, source_target_pairs={{0,1},{1,0},{2,3},{3,2},{4,5},{5,4},{6,7},{7,6},{8,9},{9,8},{10,11... | collective-permute-start | bytes 3145736 | tf_op jit(solution)/shard_map/ppermute | solution.py:38
  190.5 17.0 %collective-permute-start.52 = (f32[2,1024,128]{2,1,0:T(8,128)}, f32[2,1024,128]{2,1,0:T(8,128)S(1)}, u32[]{:S(2)}, u32[]{:S(2)}) collective-permute-start(f32[2,1024,128]{2,1,0:T(8,128)} %get-tuple-element.28), channel_id=1, source_target_pairs={{0,1},{1,0},{2,3},{3,2},{4,5},{5,4},{6,7},{7,6},{8,9},{9,8},{10,11... | collective-permute-start | bytes 3145736 | tf_op jit(solution)/shard_map/ppermute | solution.py:38
  207.1 15.2 %collective-permute-start.51 = (f32[2,1024,128]{2,1,0:T(8,128)}, f32[2,1024,128]{2,1,0:T(8,128)S(1)}, u32[]{:S(2)}, u32[]{:S(2)}) collective-permute-start(f32[2,1024,128]{2,1,0:T(8,128)} %get-tuple-element.26), channel_id=1, source_target_pairs={{0,1},{1,0},{2,3},{3,2},{4,5},{5,4},{6,7},{7,6},{8,9},{9,8},{10,11... | collective-permute-start | bytes 3145736 | tf_op jit(solution)/shard_map/ppermute | solution.py:38
  207.6 14.6 %collective-permute-start.53 = (f32[1024,128]{1,0:T(8,128)S(1)}, f32[1024,128]{1,0:T(8,128)S(1)}, u32[]{:S(2)}, u32[]{:S(2)}) collective-permute-start(f32[1024,128]{1,0:T(8,128)S(1)} %get-tuple-element.37), channel_id=1, source_target_pairs={{0,2},{1,3},{2,4},{3,5},{4,6},{5,7},{6,0},{7,1},{8,10},{9,11},{10,... | collective-permute-start | bytes 1572872 | tf_op jit(solution)/shard_map/ppermute | solution.py:34
  208.1 14.1 %collective-permute-start.57 = (f32[1024,128]{1,0:T(8,128)S(1)}, f32[1024,128]{1,0:T(8,128)S(1)}, u32[]{:S(2)}, u32[]{:S(2)}) collective-permute-start(f32[1024,128]{1,0:T(8,128)S(1)} %get-tuple-element.38), channel_id=1, source_target_pairs={{0,6},{1,7},{2,0},{3,1},{4,2},{5,3},{6,4},{7,5},{8,14},{9,15},{10,... | collective-permute-start | bytes 1572872 | tf_op jit(solution)/shard_map/ppermute | solution.py:34
  210.4 23.8 %collective-permute-start.50 = (f32[2,1024,128]{2,1,0:T(8,128)S(1)}, f32[2,1024,128]{2,1,0:T(8,128)S(1)}, u32[]{:S(2)}, u32[]{:S(2)}) collective-permute-start(f32[2,1024,128]{2,1,0:T(8,128)S(1)} %copy-done.23), channel_id=1, source_target_pairs={{0,1},{1,0},{2,3},{3,2},{4,5},{5,4},{6,7},{7,6},{8,9},{9,8},{10,11... | collective-permute-start | bytes 3145736 | tf_op jit(solution)/shard_map/ppermute | solution.py:38
  211.1 22.4 %collective-permute-start.56 = (f32[1024,128]{1,0:T(8,128)S(1)}, f32[1024,128]{1,0:T(8,128)S(1)}, u32[]{:S(2)}, u32[]{:S(2)}) collective-permute-start(f32[1024,128]{1,0:T(8,128)S(1)} %copy-done.17), channel_id=1, source_target_pairs={{0,2},{1,3},{2,4},{3,5},{4,6},{5,7},{6,0},{7,1},{8,10},{9,11},{10,... | collective-permute-start | bytes 1572872 | tf_op jit(solution)/shard_map/ppermute | solution.py:34
  222.3 11.9 %collective-permute-start.55 = (f32[1024,128]{1,0:T(8,128)S(1)}, f32[1024,128]{1,0:T(8,128)S(1)}, u32[]{:S(2)}, u32[]{:S(2)}) collective-permute-start(f32[1024,128]{1,0:T(8,128)S(1)} %copy-done.16), channel_id=1, source_target_pairs={{0,6},{1,7},{2,0},{3,1},{4,2},{5,3},{6,4},{7,5},{8,14},{9,15},{10,... | collective-permute-start | bytes 1572872 | tf_op jit(solution)/shard_map/ppermute | solution.py:34
  222.4 22.3 %collective-permute-start.54 = (f32[1024,128]{1,0:T(8,128)S(1)}, f32[1024,128]{1,0:T(8,128)S(1)}, u32[]{:S(2)}, u32[]{:S(2)}) collective-permute-start(f32[1024,128]{1,0:T(8,128)S(1)} %get-tuple-element.35), channel_id=1, source_target_pairs={{0,2},{1,3},{2,4},{3,5},{4,6},{5,7},{6,0},{7,1},{8,10},{9,11},{10,... | collective-permute-start | bytes 1572872 | tf_op jit(solution)/shard_map/ppermute | solution.py:34
  224.0 21.4 %collective-permute-start.58 = (f32[1024,128]{1,0:T(8,128)S(1)}, f32[1024,128]{1,0:T(8,128)S(1)}, u32[]{:S(2)}, u32[]{:S(2)}) collective-permute-start(f32[1024,128]{1,0:T(8,128)S(1)} %get-tuple-element.36), channel_id=1, source_target_pairs={{0,6},{1,7},{2,0},{3,1},{4,2},{5,3},{6,4},{7,5},{8,14},{9,15},{10,... | collective-permute-start | bytes 1572872 | tf_op jit(solution)/shard_map/ppermute | solution.py:34
  (32 other events, 261.2 us)
